TPU v7x, 32 devices: a whole 2x2x4 slice. The times are simulated.
32 devices in a mesh: batch: 4 (over x, core), seq: 8 (over z, y).
Axes of the slice: x: 2, y: 2, z: 4, core: 2. Of those that a mesh axis runs over, the one named last changes fastest.
Arguments:
- inputs: bfloat16 [8, 2048, 512], P('batch', 'seq'), may hold values from -6 to 6
- lengths: int32 [8], P('batch'), may hold values from 1 to 2048, 10240 in all
- conv_taps: bfloat16 [512, 9], P(('batch', 'seq')), may hold values from -4 to 4
- gain_attn: bfloat16 [512], P(('batch', 'seq')), may hold values from 0.5 to 1.5
- w_proj: bfloat16 [512, 512], P(('batch', 'seq')), may hold values from -0.25 to 0.25
- w_query: bfloat16 [512, 512], P(('batch', 'seq')), may hold values from -0.03125 to 0.03125
- w_key: bfloat16 [512, 512], P(('batch', 'seq')), may hold values from -0.25 to 0.25
- w_value: bfloat16 [512, 512], P(('batch', 'seq')), may hold values from -0.25 to 0.25
- w_out: bfloat16 [512, 512], P(('batch', 'seq')), may hold values from -2 to 2
- gain_ffn: bfloat16 [512], P(('batch', 'seq')), may hold values from 0.5 to 1.5
- w_gate: bfloat16 [512, 2048], P(('batch', 'seq')), may hold values from -0.25 to 0.25
- w_up: bfloat16 [512, 2048], P(('batch', 'seq')), may hold values from -0.25 to 0.25
- w_down: bfloat16 [2048, 512], P(('batch', 'seq')), may hold values from -0.125 to 0.125
- rel_bias: bfloat16 [256], P(('batch', 'seq')), may hold values from -4 to 4
- cotangent: bfloat16 [8, 2048, 512], P('batch', 'seq'), may hold values from -6 to 6
Outputs:
- layer_out: bfloat16 [8, 2048, 512], P('batch', 'seq')
- input_grad: bfloat16 [8, 2048, 512], P('batch', 'seq')
- grad_taps: float32 [512, 9], P(('batch', 'seq'))
- grad_gain_attn: float32 [512], P(('batch', 'seq'))
- grad_proj: float32 [512, 512], P(('batch', 'seq'))
- grad_query: float32 [512, 512], P(('batch', 'seq'))
- grad_key: float32 [512, 512], P(('batch', 'seq'))
- grad_value: float32 [512, 512], P(('batch', 'seq'))
- grad_out: float32 [512, 512], P(('batch', 'seq'))
- grad_gain_ffn: float32 [512], P(('batch', 'seq'))
- grad_gate: float32 [512, 2048], P(('batch', 'seq'))
- grad_up: float32 [512, 2048], P(('batch', 'seq'))
- grad_down: float32 [2048, 512], P(('batch', 'seq'))
- grad_rel_bias: float32 [256], P(('batch', 'seq'))
Inputs may be any that keep to these rules, and one draw needn't show every extreme that they name: Sequence s holds lengths[s] valid bytes at its start, the rest is padding; some sequence has all 2048 bytes valid.
All inputs are finite; a program needn't handle non-finite values. No bound on the sum of `lengths` on one device may be relied on, other than what follows from the above.
Results may differ from a plain program's by a relative error of at most 0.035.
Values may be sent and summed in bfloat16 or wider, within the bound.
A program may use at most 256 MiB of HBM per device.

v0:
```python
import functools
from functools import partial

import jax
import jax.numpy as jnp
import numpy as np
from jax import lax
from jax.experimental import pallas as pl
from jax.experimental.pallas import tpu as pltpu
from jax.sharding import PartitionSpec as P

NB = 32
EPSILON = 1e-06
LIMITS = (12, 16, 23, 32, 46, 64, 91)
WINDOWS = ((2, 0), (3, 2), (4, 5))
TAPS = 9
PACK = 128
SPAN = 8

def mat_dot(lhs_array, rhs_array):
    return jnp.dot(lhs_array, rhs_array, preferred_element_type=jnp.float32)


def outer_sum(lhs_array, rhs_array):
    return lax.dot_general(
        lhs_array, rhs_array, (((0,), (0,)), ((), ())), preferred_element_type=jnp.float32
    )


def back_dot(grad_rows, weight):
    return lax.dot_general(
        grad_rows, weight, (((1,), (1,)), ((), ())), preferred_element_type=jnp.float32
    )


def bucket_of(relative):
    distance = jnp.abs(relative)
    larger = jnp.full(relative.shape, 8, jnp.int32)
    for threshold in LIMITS:
        larger = larger + (distance >= threshold).astype(jnp.int32)
    inside = jnp.where(distance < 8, distance, larger)
    return inside + 16 * (relative > 0).astype(jnp.int32)


def norm_rows(hidden, gain_row):
    return (
        hidden * lax.rsqrt(jnp.mean(hidden * hidden, axis=-1, keepdims=True) + EPSILON) * gain_row
    )


def gated(gate_pre, up_pre):
    return jax.nn.gelu(gate_pre, approximate=True) * up_pre


def conv_mix(padded, taps, row_count):
    summed = jnp.zeros(padded.shape[:-2] + (row_count, padded.shape[-1]), jnp.float32)
    for window_len, offset in WINDOWS:
        conv_sum = jnp.zeros_like(summed)
        for tap_index in range(window_len):
            shifted = lax.slice_in_dim(
                padded, 3 - tap_index, 3 - tap_index + row_count, axis=padded.ndim - 2
            )
            conv_sum = conv_sum + taps[:, offset + tap_index] * shifted
        summed = summed + jax.nn.gelu(conv_sum, approximate=True)
    return summed


def near_offsets(rows):
    lane = np.arange(2 * rows)
    lane = np.where(lane < rows, lane, lane - 2 * rows)
    return rows * (np.arange(3)[:, None, None] - 1) + np.arange(8)[None, :, None] - lane[None, None, :]


def bias_tables(table, rows):
    heads = table.shape[0]
    buckets = bucket_of(jnp.asarray(near_offsets(rows)[:, 0, :], jnp.int32)).reshape(-1)
    onehot = (buckets[None, :] == jnp.arange(NB, dtype=jnp.int32)[:, None]).astype(jnp.float32)
    diag = jnp.dot(table, onehot, precision=lax.Precision.HIGHEST)
    far = jnp.stack([table[:, NB // 2 - 1], table[:, NB - 1]], axis=1)
    return far, diag.reshape(heads // 2, 6, 2 * rows)


def bias_grad(near, rows):
    near = near.reshape(near.shape[0] * 2, 5, 8, 2 * rows)
    buckets = bucket_of(jnp.asarray(near_offsets(rows), jnp.int32))
    hit = buckets[None] == jnp.arange(NB, dtype=jnp.int32)[:, None, None, None]
    grad = jnp.sum(jnp.where(hit[None], near[:, None, 1:4], 0.0), axis=(2, 3, 4))
    left = jnp.sum(near[:, 0], axis=(1, 2))
    right = jnp.sum(near[:, 4], axis=(1, 2))
    return grad.at[:, NB // 2 - 1].add(left).at[:, NB - 1].add(right)


def nt_dot(a, b):
    return lax.dot_general(a, b, (((1,), (1,)), ((), ())), preferred_element_type=jnp.float32)


def tn_dot(a, b):
    return lax.dot_general(a, b, (((0,), (0,)), ((), ())), preferred_element_type=jnp.float32)


def nn_dot(a, b):
    return lax.dot_general(a, b, (((1,), (0,)), ((), ())), preferred_element_type=jnp.float32)


def fill_bias(rows, far_ref, diag_ref, bias_ref, pair):
    for a in range(2):
        bias_ref[a, 0] = jnp.full((rows, rows), far_ref[2 * pair + a, 0], jnp.float32)
        bias_ref[a, 4] = jnp.full((rows, rows), far_ref[2 * pair + a, 1], jnp.float32)
        for c in range(3):
            base = jnp.broadcast_to(diag_ref[0, 3 * a + c : 3 * a + c + 1, :], (rows, 2 * rows))
            bias_ref[a, 1 + c] = pltpu.roll(base, 0, 1, stride=1, stride_axis=0)[:, :rows]


def head_halves(block):
    lane = lax.broadcasted_iota(jnp.int32, block.shape, 1)
    zero = jnp.zeros_like(block)
    half = block.shape[1] // 2
    return jnp.where(lane < half, block, zero), jnp.where(lane < half, zero, block)


def attend_kernel(
    rows, info_ref, far_ref, diag_ref, q_ref, k_ref, v_ref, o_ref, full_ref, inv_ref, peak_ref, bias_ref, s_ref, acc_ref
):
    pair, b = pl.program_id(0), pl.program_id(1)

    @pl.when(b == 0)
    def _():
        fill_bias(rows, far_ref, diag_ref, bias_ref, pair)

    length, first = info_ref[b], info_ref[pl.num_programs(1)]
    count = lax.div(length + rows - 1, rows)
    halves = head_halves(q_ref[...])
    wide = q_ref.shape[1]
    half = wide // 2
    key_row = lax.broadcasted_iota(jnp.int32, (rows, rows), 0)

    def scores(kc, peaks):
        k = k_ref[0, pl.ds(kc * rows, SPAN * rows), :]
        new = list(peaks)
        for a in range(2):
            full = nt_dot(k, halves[a])
            for u in range(SPAN):
                slot = jnp.clip(kc + u - first + 2, 0, 4)
                valid = key_row < length - (kc + u) * rows
                s = full[u * rows : (u + 1) * rows] + bias_ref[a, slot]
                s = jnp.where(valid, s, -1e9)
                s_ref[a, pl.ds((kc + u) * rows, rows), :] = s
                new[a] = jnp.maximum(new[a], jnp.max(s.reshape(rows // 8, 8, rows), axis=0))
        return tuple(new)

    low = jnp.full((8, rows), -jnp.inf, jnp.float32)
    spans = lax.div(count + SPAN - 1, SPAN)
    peaks = lax.fori_loop(0, spans, lambda i, p: scores(i * SPAN, p), (low, low))
    peaks = [jnp.max(p, axis=0, keepdims=True) for p in peaks]
    acc_ref[...] = jnp.zeros_like(acc_ref)
    lane = lax.broadcasted_iota(jnp.int32, (SPAN * rows, wide), 1)

    def weigh(i, carry):
        here = pl.ds(i * SPAN * rows, SPAN * rows)
        v = v_ref[0, here, :]
        ones = jnp.ones_like(v)
        for a, v_one in enumerate((jnp.where(lane < half, v, ones), jnp.where(lane < half, ones, v))):
            e = jnp.exp(s_ref[a, here, :] - peaks[a])
            acc_ref[a] += tn_dot(v_one, e.astype(jnp.bfloat16))
        return carry

    lax.fori_loop(0, spans, weigh, 0)
    inv = jnp.concatenate([1.0 / acc_ref[0, half:], 1.0 / acc_ref[1, :half]], axis=0)
    out = jnp.concatenate([acc_ref[0, :half], acc_ref[1, half:]], axis=0) * inv
    out = out.T
    o_ref[...] = out.astype(o_ref.dtype)
    full_ref[...] = out
    inv_ref[...] = inv.T
    for a in range(2):
        peak_ref[0, 0, a : a + 1, :] = peaks[a]


def attention_cost(q, kv, products):
    flops = products * 8 * q.shape[0] * kv.shape[1] * q.shape[1]
    return pl.CostEstimate(
        flops=flops, bytes_accessed=2 * (q.size + kv.size) * products, transcendentals=8 * q.shape[0] * kv.shape[1]
    )


def attend(info, far, diag, q, kv, rows, length):
    heads = far.shape[0]
    seqs = kv.shape[0]
    wide = 2 * (q.shape[1] // heads)
    pairs = heads // 2
    smem = pl.BlockSpec(memory_space=pltpu.SMEM)
    return pl.pallas_call(
        functools.partial(attend_kernel, rows),
        grid=(pairs, seqs),
        in_specs=[
            smem, smem,
            pl.BlockSpec((1, 6, 2 * rows), lambda p, b: (p, 0, 0)),
            pl.BlockSpec((rows, wide), lambda p, b: (b, p)),
            pl.BlockSpec((1, length, wide), lambda p, b: (b, 0, 2 * p)),
            pl.BlockSpec((1, length, wide), lambda p, b: (b, 0, 2 * p + 1)),
        ],
        out_specs=[pl.BlockSpec((rows, wide), lambda p, b: (b, p))] * 3
        + [pl.BlockSpec((1, 1, 2, rows), lambda p, b: (b, p, 0, 0))],
        out_shape=[
            jax.ShapeDtypeStruct(q.shape, jnp.bfloat16),
            jax.ShapeDtypeStruct(q.shape, jnp.float32),
            jax.ShapeDtypeStruct(q.shape, jnp.float32),
            jax.ShapeDtypeStruct((seqs, pairs, 2, rows), jnp.float32),
        ],
        scratch_shapes=[
            pltpu.VMEM((2, 5, rows, rows), jnp.float32),
            pltpu.VMEM((2, length, rows), jnp.float32),
            pltpu.VMEM((2, wide, rows), jnp.float32),
        ],
        compiler_params=pltpu.CompilerParams(vmem_limit_bytes=48 << 20),
        cost_estimate=attention_cost(q, kv, 2),
        name="attend",
    )(info, far, diag, q, kv, kv)


def back_pair(rows, length, first, q, g, full, key_value, peak, bias_ref, sum_ref, acc_ref, write):
    q_half, g_half = head_halves(q), head_halves(g)
    wide = q.shape[1]
    half = wide // 2
    key_row = lax.broadcasted_iota(jnp.int32, (rows, rows), 0)
    acc_ref[...] = jnp.zeros_like(acc_ref)
    along = (g.astype(jnp.float32) * full).T
    delta = [jnp.sum(along[a * half : (a + 1) * half], axis=0, keepdims=True) for a in range(2)]
    keys, spans = key_value

    def step(i, carry):
        kc = i * SPAN
        here = pl.ds(kc * rows, SPAN * rows)
        k, v = keys(here)
        dk = dv = None
        for a in range(2):
            s = nt_dot(k, q_half[a])
            dp = nt_dot(v, g_half[a])
            es, dss = [], []
            for u in range(SPAN):
                part = slice(u * rows, (u + 1) * rows)
                slot = jnp.clip(kc + u - first + 2, 0, 4)
                valid = key_row < length - (kc + u) * rows
                e = jnp.exp(s[part] + bias_ref[a, slot] - peak[a])
                e_low = jnp.where(valid, e, 0.0).astype(jnp.bfloat16)
                ds = e_low.astype(jnp.float32) * (dp[part] - delta[a])
                sum_ref[a, slot] += ds
                es.append(e_low)
                dss.append(ds.astype(jnp.bfloat16))
            e_low, ds_low = jnp.concatenate(es, axis=0), jnp.concatenate(dss, axis=0)
            dv_a = nn_dot(e_low, g_half[a])
            dk_a = nn_dot(ds_low, q_half[a])
            dv = dv_a if dv is None else dv + dv_a
            dk = dk_a if dk is None else dk + dk_a
            acc_ref[a] += tn_dot(k, ds_low)
        write(here, dk.astype(jnp.bfloat16), dv.astype(jnp.bfloat16))
        return carry

    if spans == 1:
        step(0, 0)
    else:
        lax.fori_loop(0, spans, step, 0)
    return jnp.concatenate([acc_ref[0, :half], acc_ref[1, half:]], axis=0).T.astype(jnp.bfloat16)


def near_sums(rows, sum_ref, write):
    for a in range(2):
        for slot in range(5):
            total_sum = jnp.zeros((8, 2 * rows), jnp.float32)
            for g in range(rows // 8):
                part = jnp.concatenate(
                    [sum_ref[a, slot, 8 * g : 8 * g + 8, :], jnp.zeros((8, rows), jnp.float32)], axis=1
                )
                if g and 0 < slot < 4:
                    part = pltpu.roll(part, 2 * rows - 8 * g, 1)
                total_sum = total_sum + part
            write(a, slot, total_sum)


def attend_back_kernel(rows, info_ref, far_ref, diag_ref, q_ref, g_ref, full_ref, k_ref, v_ref, peak_ref,
                       dq_ref, dkv_ref, near_ref, bias_ref, sum_ref, acc_ref):
    pair, b = pl.program_id(0), pl.program_id(1)

    @pl.when(b == 0)
    def _():
        fill_bias(rows, far_ref, diag_ref, bias_ref, pair)
        sum_ref[...] = jnp.zeros_like(sum_ref)

    wide = q_ref.shape[1]

    def write(here, dk, dv):
        dkv_ref[0, here, :wide] = dk
        dkv_ref[0, here, wide:] = dv

    dq_ref[...] = back_pair(
        rows,
        info_ref[b],
        info_ref[info_ref.shape[0] - 1],
        q_ref[...],
        g_ref[...],
        full_ref[...],
        (lambda here: (k_ref[0, here, :], v_ref[0, here, :]), k_ref.shape[1] // (SPAN * rows)),
        [peak_ref[0, 0, a : a + 1, :] for a in range(2)],
        bias_ref,
        sum_ref,
        acc_ref,
        write,
    )

    @pl.when(b == pl.num_programs(1) - 1)
    def _():
        def keep(a, slot, value):
            near_ref[0, a, slot] = value

        near_sums(rows, sum_ref, keep)


def attend_back(info, far, diag, q, g, full, kv, peak, rows, length, seqs):
    heads = far.shape[0]
    wide = 2 * (q.shape[1] // heads)
    pairs = heads // 2
    smem = pl.BlockSpec(memory_space=pltpu.SMEM)
    row_spec = pl.BlockSpec((rows, wide), lambda p, b: (b, p))
    return pl.pallas_call(
        functools.partial(attend_back_kernel, rows),
        grid=(pairs, seqs),
        in_specs=[
            smem,
            smem,
            pl.BlockSpec((1, 6, 2 * rows), lambda p, b: (p, 0, 0)),
            row_spec,
            row_spec,
            row_spec,
            pl.BlockSpec((1, length, wide), lambda p, b: (b, 0, 2 * p)),
            pl.BlockSpec((1, length, wide), lambda p, b: (b, 0, 2 * p + 1)),
            pl.BlockSpec((1, 1, 2, rows), lambda p, b: (b, p, 0, 0)),
        ],
        out_specs=[
            row_spec,
            pl.BlockSpec((1, length, 2 * wide), lambda p, b: (b, 0, p)),
            pl.BlockSpec((1, 2, 5, 8, 2 * rows), lambda p, b: (p, 0, 0, 0, 0)),
        ],
        out_shape=[
            jax.ShapeDtypeStruct((seqs * rows, q.shape[1]), jnp.bfloat16),
            jax.ShapeDtypeStruct((seqs,) + kv.shape[1:], jnp.bfloat16),
            jax.ShapeDtypeStruct((pairs, 2, 5, 8, 2 * rows), jnp.float32),
        ],
        scratch_shapes=[
            pltpu.VMEM((2, 5, rows, rows), jnp.float32),
            pltpu.VMEM((2, 5, rows, rows), jnp.float32),
            pltpu.VMEM((2, wide, rows), jnp.float32),
        ],
        compiler_params=pltpu.CompilerParams(vmem_limit_bytes=48 << 20),
        cost_estimate=attention_cost(q, kv, 3),
        name="attend_back",
    )(info, far, diag, q, g, full, kv, kv, peak)


SLOTS = ("x", "c", "z", "y")
MESH = pl.DeviceIdType.MESH


def layout_of(batch, seq):
    fast = 1 << ((seq.bit_length() - 1) // 2)
    return {"x": batch // 2, "c": 2, "z": seq // fast, "y": fast}


def tile_block(rows, cols):
    return (rows, cols) if rows % 16 == 0 else (rows * cols // 128, 128)


def place(sizes):
    b, s = lax.axis_index("batch"), lax.axis_index("seq")
    return {
        "x": lax.div(b, 2),
        "c": lax.rem(b, 2),
        "z": lax.div(s, sizes["y"]),
        "y": lax.rem(s, sizes["y"]),
    }


def device_at(sizes, me, dim, at):
    spot = dict(me)
    spot[dim] = at
    return (spot["x"] * 2 + spot["c"], spot["z"] * sizes["y"] + spot["y"])


def seq_peer(sizes, me, k):
    n = sizes["z"] * sizes["y"]
    return (me["x"] * 2 + me["c"], lax.rem(me["z"] * sizes["y"] + me["y"] + k, n))


def greet(sizes, me, dims):
    barrier = pltpu.get_barrier_semaphore()
    total = 0
    if "s" in dims:
        total = sizes["z"] * sizes["y"] - 1
        for k in range(1, total + 1):
            pl.semaphore_signal(barrier, inc=1, device_id=seq_peer(sizes, me, k), device_id_type=MESH)
        dims = [d for d in dims if d not in "szy"]
    for dim in dims:
        for k in range(1, sizes[dim]):
            peer = device_at(sizes, me, dim, lax.rem(me[dim] + k, sizes[dim]))
            pl.semaphore_signal(barrier, inc=1, device_id=peer, device_id_type=MESH)
            total += 1
    pl.semaphore_wait(barrier, total)


class Sems:
    def __init__(self, send, recv):
        self.send, self.recv, self.used = send, recv, 0

    def take(self, count):
        first = self.used
        self.used += count
        assert self.used <= self.send.shape[0]
        return first

    def copy(self, src, dst, index, device):
        return pltpu.make_async_remote_copy(
            src_ref=src, dst_ref=dst, send_sem=self.send.at[index], recv_sem=self.recv.at[index],
            device_id=device, device_id_type=MESH,
        )


def run_together(tasks, plan=()):
    tasks = list(tasks)
    over_already = set()
    for i in plan:
        if i not in over_already:
            try:
                next(tasks[i])
            except StopIteration:
                over_already.add(i)
    tasks = [t for i, t in enumerate(tasks) if i not in over_already]
    while tasks:
        left = []
        for task in tasks:
            try:
                next(task)
                left.append(task)
            except StopIteration:
                pass
        tasks = left


def gather_task(sizes, me, src, out, local_sem, sems, order):
    before = list(SLOTS[len(SLOTS) - (len(src.shape) - 2) :])
    dims = [d for d in SLOTS if d in order.lower() or d in before]
    own = pltpu.make_async_copy(src, out.at[tuple(me[d] for d in dims if d not in before)], local_sem)
    own.start()
    own.wait()
    done = before
    sent = []
    for dim in order:
        direct, dim = dim.isupper(), dim.lower()
        n, at = sizes[dim], me[dim]

        def region(origin):
            spots = []
            for d in dims:
                spots.append(slice(None) if d in done else (origin if d == dim else me[d]))
            return out.at[tuple(spots)]

        if n == 2:
            base = sems.take(1)
            other = 1 - at
            send = sems.copy(region(at), region(at), base, device_at(sizes, me, dim, other))
            send.start()
            yield
            sems.copy(region(other), region(other), base, device_at(sizes, me, dim, other)).wait_recv()
            sent.append((None, send))
        elif direct:
            base = sems.take(n - 1)
            for k in range(1, n):
                peer = device_at(sizes, me, dim, lax.rem(at + k, n))
                send = sems.copy(region(at), region(at), base + k - 1, peer)
                send.start()
                sent.append((None, send))
            yield
            for k in range(1, n):
                origin = lax.rem(at + n - k, n)
                sems.copy(region(origin), region(origin), base + k - 1, device_at(sizes, me, dim, origin)).wait_recv()
        else:
            for t in range(n - 1):
                base = sems.take(2)
                to_right = (at + 1 < n) & (at - t >= 0)
                to_left = (at >= 1) & (at + t < n)
                from_left = (at >= 1) & (at - 1 - t >= 0)
                from_right = (at + 1 < n) & (at + 1 + t < n)
                right = sems.copy(region(at - t), region(at - t), base, device_at(sizes, me, dim, at + 1))
                left = sems.copy(region(at + t), region(at + t), base + 1, device_at(sizes, me, dim, at - 1))
                pl.when(to_right)(right.start)
                pl.when(to_left)(left.start)
                sent += [(to_right, right), (to_left, left)]
                yield
                got = sems.copy(region(at - 1 - t), region(at - 1 - t), base, device_at(sizes, me, dim, at - 1))
                pl.when(from_left)(got.wait_recv)
                got = sems.copy(region(at + 1 + t), region(at + 1 + t), base + 1, device_at(sizes, me, dim, at + 1))
                pl.when(from_right)(got.wait_recv)
        done.append(dim)
    for cond, send in sent:
        if cond is None:
            send.wait_send()
        else:
            pl.when(cond)(send.wait_send)


def spread_task(sizes, me, src, out, local_sem, sems):
    z, y, n, fast = me["z"], me["y"], sizes["z"], sizes["y"]
    own = pltpu.make_async_copy(src, out.at[:, z, y], local_sem)
    own.start()
    own.wait()
    fan = sems.take((fast - 1) * n)

    def fan_copy(k, origin, owner):
        peer = device_at(sizes, me, "y", lax.rem(y + k, fast))
        spot = out.at[:, origin, owner]
        return sems.copy(spot, spot, fan + (k - 1) * n + origin, peer)

    def fan_out(origin):
        for k in range(1, fast):
            fan_copy(k, origin, y).start()

    fan_out(z)
    sent = []
    for t in range(n - 1):
        base = sems.take(2)
        to_right = (z + 1 < n) & (z - t >= 0)
        to_left = (z >= 1) & (z + t < n)
        from_left = (z >= 1) & (z - 1 - t >= 0)
        from_right = (z + 1 < n) & (z + 1 + t < n)
        right = sems.copy(out.at[:, z - t, y], out.at[:, z - t, y], base, device_at(sizes, me, "z", z + 1))
        left = sems.copy(out.at[:, z + t, y], out.at[:, z + t, y], base + 1, device_at(sizes, me, "z", z - 1))
        pl.when(to_right)(right.start)
        pl.when(to_left)(left.start)
        sent += [(to_right, right), (to_left, left)]
        yield

        @pl.when(from_left)
        def _():
            spot = out.at[:, z - 1 - t, y]
            sems.copy(spot, spot, base, device_at(sizes, me, "z", z - 1)).wait_recv()
            fan_out(z - 1 - t)

        @pl.when(from_right)
        def _():
            spot = out.at[:, z + 1 + t, y]
            sems.copy(spot, spot, base + 1, device_at(sizes, me, "z", z + 1)).wait_recv()
            fan_out(z + 1 + t)

    yield
    for k in range(1, fast):
        for origin in range(n):
            fan_copy(k, origin, lax.rem(y + fast - k, fast)).wait_recv()
    for k in range(1, fast):
        for origin in range(n):
            fan_copy(k, origin, y).wait_send()
    for cond, send in sent:
        pl.when(cond)(send.wait_send)


def shift_task(sizes, me, src, out, sems, step):
    n = sizes["z"] * sizes["y"]
    s = me["z"] * sizes["y"] + me["y"]
    base = sems.take(1)
    send = sems.copy(src, out, base, seq_peer(sizes, me, step % n))
    has_to = (s < n - 1) if step > 0 else (s > 0)
    has_from = (s > 0) if step > 0 else (s < n - 1)
    pl.when(has_to)(send.start)
    yield
    pl.when(has_from)(send.wait_recv)

    @pl.when(jnp.logical_not(has_from))
    def _():
        out[...] = jnp.zeros_like(out)

    yield
    pl.when(has_to)(send.wait_send)


def stage_count(sizes, order):
    return sum(1 if sizes[d] == 2 else 2 * (sizes[d] - 1) for d in order.lower())


def gather_kernel(sizes, orders, has_rows, has_rim, plan, *refs):
    count = len(orders)
    total = count + has_rows + has_rim
    ins, outs = refs[:total], refs[total : 2 * total]
    local_sem, send_sem, recv_sem = refs[2 * total :]
    me = place(sizes)
    used = [d for d in SLOTS if any(d in o.lower() for o in orders) or (has_rows and d in "zy")]
    greet(sizes, me, used + ["s"] * has_rim)
    sems = Sems(send_sem, recv_sem)
    tasks = []
    for i in range(count):
        tasks.append(gather_task(sizes, me, ins[i], outs[i], local_sem.at[i], sems, orders[i]))
    if has_rows:
        tasks.append(spread_task(sizes, me, ins[count], outs[count], local_sem.at[count], sems))
    if has_rim:
        tasks.append(shift_task(sizes, me, ins[-1], outs[-1], sems, 1))
    run_together(tasks, plan)


def gather_all(shards, orders, sizes, collective_id, rows=None, rim=None, plan=(), name="gather"):
    ins, shapes, out_specs = [], [], []
    for shard, order in zip(shards, orders):
        ins.append(shard if shard.ndim > 2 else shard.reshape(tile_block(*shard.shape)))
        before = SLOTS[len(SLOTS) - (ins[-1].ndim - 2) :]
        whole = tuple(sizes[d] for d in SLOTS if d in order.lower() or d in before)
        shapes.append(jax.ShapeDtypeStruct(whole + ins[-1].shape[-2:], shard.dtype))
    total = sum(stage_count(sizes, o) for o in orders)
    out_specs = [pl.BlockSpec(memory_space=pl.ANY)] * len(ins)
    if rows is not None:
        ins.append(rows)
        shapes.append(jax.ShapeDtypeStruct((rows.shape[0], sizes["z"], sizes["y"]) + rows.shape[1:], rows.dtype))
        out_specs.append(pl.BlockSpec(memory_space=pl.ANY))
        total += (sizes["y"] - 1) * sizes["z"] + 2 * (sizes["z"] - 1)
    if rim is not None:
        ins.append(rim)
        shapes.append(jax.ShapeDtypeStruct(rim.shape, rim.dtype))
        out_specs.append(pl.BlockSpec(memory_space=pltpu.VMEM))
        total += 1
    return pl.pallas_call(
        functools.partial(gather_kernel, sizes, orders, int(rows is not None), int(rim is not None), plan),
        in_specs=[pl.BlockSpec(memory_space=pltpu.VMEM)] * len(ins),
        out_specs=out_specs,
        out_shape=shapes,
        scratch_shapes=[
            pltpu.SemaphoreType.DMA((len(ins),)),
            pltpu.SemaphoreType.DMA((total,)),
            pltpu.SemaphoreType.DMA((total,)),
        ],
        compiler_params=pltpu.CompilerParams(collective_id=collective_id, has_side_effects=True),
        name=name,
    )(*ins)


def over(extents, body):
    total = 1
    for e in extents:
        total *= e
    if total == 1:
        body((0,) * len(extents))
        return

    def step(i, carry):
        spots = []
        for e in reversed(extents):
            spots.append(lax.rem(i, e))
            i = lax.div(i, e)
        body(tuple(reversed(spots)))
        return carry

    lax.fori_loop(0, total, step, 0)


def add_into(dst, src_of, extents):
    def body(spots):
        here = spots + (slice(None), slice(None))
        dst[here] = (dst[here].astype(jnp.float32) + src_of(spots).astype(jnp.float32)).astype(dst.dtype)

    over(extents, body)


def add_pair(out, first, second_of, extents):
    def body(spots):
        here = spots + (slice(None), slice(None))
        out[here] = (first[here].astype(jnp.float32) + second_of(spots).astype(jnp.float32)).astype(out.dtype)

    over(extents, body)


def reduce_task(sizes, me, src, out, bufs, sems, order, dims):
    remaining = list(dims)
    current = src
    stages = []
    for stage, dim in enumerate(order):
        last = stage == len(order) - 1
        if dim == "s":
            n, s = sizes["z"] * sizes["y"], me["z"] * sizes["y"] + me["y"]
            base = sems.take(n)
            sends, recvs = [], []
            for k in range(1, n):
                to = lax.rem(s + k, n)
                spot = current.at[lax.div(to, sizes["y"]), lax.rem(to, sizes["y"])]
                sends.append(sems.copy(spot, bufs[stage].at[k], base + k, seq_peer(sizes, me, k)))
                recvs.append(sems.copy(bufs[stage].at[k], bufs[stage].at[k], base + k, seq_peer(sizes, me, k)))
            stages.append((dim, n, current, bufs[stage], sends, recvs, None, None, None))
            continue
        direct, dim = dim.isupper(), dim.lower()
        n, at = sizes[dim], me[dim]
        spot = remaining.index(dim)
        remaining.remove(dim)
        extents = [sizes[d] for d in remaining]

        def block(j, source=current, spot=spot):
            return source.at[(slice(None),) * spot + (j,)]

        def values(j, source=current, spot=spot):
            return lambda spots: source[spots[:spot] + (j,) + spots[spot:] + (slice(None), slice(None))]

        if direct:
            base = sems.take(n)
            moves = []
            for k in range(1, n):
                to, origin = lax.rem(at + k, n), lax.rem(at + n - k, n)
                buf = bufs[stage].at[k]
                send = sems.copy(block(to), buf, base + k, device_at(sizes, me, dim, to))
                moves.append((send, sems.copy(buf, buf, base + k, device_at(sizes, me, dim, origin))))
            result = out if last else bufs[stage].at[0]
            stages.append(("direct", n, result, bufs[stage], moves, at, values, extents, last))
            current = result
        elif n == 2:
            send = sems.copy(block(1 - at), bufs[stage], sems.take(1), device_at(sizes, me, dim, 1 - at))
            stages.append((dim, n, None, bufs[stage], [send], at, values, extents, last))
            current = bufs[stage]
        else:
            chains = bufs[stage][0]
            result = out if last else bufs[stage][1]
            base = sems.take(2 * n)
            moves = []
            for slot in range(n - 1):
                for side in range(2):
                    lead = at if side == 0 else n - 1 - at
                    j = lax.rem((n - 1 - slot + at) if side == 0 else (slot + 1 + at + n), n)
                    buf = chains.at[side, j]
                    to = device_at(sizes, me, dim, at + 1 if side == 0 else at - 1)
                    index = base + side * n + j
                    plain, summed = sems.copy(block(j), buf, index, to), sems.copy(buf, buf, index, to)
                    moves.append((plain, summed, buf, j, lead == 0, (lead > 0) & (lead <= slot), lead <= slot))
            ends = []
            for side in range(2):
                buf = chains.at[side, at]
                ends.append(sems.copy(buf, buf, base + side * n + at, device_at(sizes, me, dim, at)))
            conds = (at > 0, at < n - 1)
            stages.append((dim, n, result, chains, moves, at, values, extents, (ends, conds)))
            current = result

    for dim, n, source, buf, moves, at, values, extents, last in stages:
        if dim == "s":
            for send in moves:
                send.start()
            yield
            total = source[me["z"], me["y"]].astype(jnp.float32)
            for k in range(1, n):
                at[k - 1].wait_recv()
                total = total + buf[k].astype(jnp.float32)
            out[...] = total
        elif dim == "direct":
            for send, _ in moves:
                send.start()
            yield
            for _, got in moves:
                got.wait_recv()

            def add_all(spots):
                here = spots + (slice(None), slice(None))
                total = values(at)(spots).astype(jnp.float32)
                for k in range(1, n):
                    total = total + buf[(k,) + here].astype(jnp.float32)
                source[here] = total.astype(source.dtype)

            over(extents, add_all)
        elif n == 2:
            moves[0].start()
            yield
            moves[0].wait_recv()
            if last:
                add_pair(out, buf, values(at), extents)
            else:
                add_into(buf, values(at), extents)
        else:
            for slot in range(n - 1):
                for plain, summed, target, j, is_first, is_later, _ in moves[2 * slot : 2 * slot + 2]:

                    def pass_on(summed=summed, target=target, j=j):
                        summed.wait_recv()
                        add_into(target, values(j), extents)
                        summed.start()

                    pl.when(is_first)(plain.start)
                    pl.when(is_later)(pass_on)
                yield

            def start(spots):
                here = spots + (slice(None), slice(None))
                source[here] = values(at)(spots).astype(source.dtype)

            over(extents, start)
            ends, conds = last
            for side in range(2):

                def finish(side=side):
                    ends[side].wait_recv()
                    add_into(source, lambda spots: buf[(side, at) + spots + (slice(None), slice(None))], extents)

                pl.when(conds[side])(finish)
    for dim, n, _, _, moves, _, _, _, _ in stages:
        for move in moves:
            if dim == "direct":
                move[0].wait_send()
            elif dim == "s" or n == 2:
                move.wait_send()
            else:
                pl.when(move[-1])(move[1].wait_send)


class Split:
    def __init__(self, parts):
        self.parts = parts
        self.dtype = parts[0].dtype

    def __setitem__(self, here, value):
        first = 0
        for part in self.parts:
            last = first + part.shape[-1]
            part[here] = value[:, first:last]
            first = last

    def __getitem__(self, here):
        return jnp.concatenate([part[here] for part in self.parts], axis=1)


def stage_buffers(sizes, block, dtype, dims, order):
    scratch, counts, left, total = [], [], list(dims), 0
    for dim in order:
        counts.append(1)
        if dim == "s":
            left = []
            n = sizes["z"] * sizes["y"]
            scratch.append(pltpu.VMEM((n,) + block, dtype))
            total += n
            continue
        left.remove(dim.lower())
        shape = tuple(sizes[d] for d in left) + block
        n = sizes[dim.lower()]
        if dim.isupper():
            scratch.append(pltpu.VMEM((n,) + shape, dtype))
            total += n
        elif n == 2:
            scratch.append(pltpu.VMEM(shape, dtype))
            total += 1
        else:
            scratch.append(pltpu.VMEM((2, n) + shape, dtype))
            total += 2 * n
            if dim != order[-1]:
                scratch.append(pltpu.VMEM(shape, dtype))
                counts[-1] = 2
    return scratch, counts, total, left


def stage_refs(sizes, order, counts, bufs):
    stages = []
    for dim, size in zip(order, counts):
        taken = [bufs.pop(0) for _ in range(size)]
        stages.append(taken[0] if dim == "s" or dim.isupper() or sizes[dim] == 2 else taken)
    return stages


def reduce_kernel(sizes, orders, dims, counts, splits, spill, *refs):
    count = len(orders)
    total = count + spill
    ends = sum(splits) + spill
    ins, outs = refs[:total], list(refs[total : total + ends])
    send_sem, recv_sem = refs[-2:]
    bufs = list(refs[total + ends : -2])
    me = place(sizes)
    used = [d for d in SLOTS if any(d in o.lower() for o in orders)]
    greet(sizes, me, used + ["s"] * (spill or any("s" in o for o in orders)))
    sems = Sems(send_sem, recv_sem)
    tasks = []
    for i in range(count):
        stages = stage_refs(sizes, orders[i], counts[i], bufs)
        parts = [outs.pop(0) for _ in range(splits[i])]
        out = parts[0] if len(parts) == 1 else Split(parts)
        tasks.append(reduce_task(sizes, me, ins[i], out, stages, sems, orders[i], dims[i]))
    if spill:
        tasks.insert(0, shift_task(sizes, me, ins[-1], outs.pop(0), sems, -1))
    run_together(tasks)


def cut_shapes(block, left, widths, sizes, dtype):
    if left or widths is None or sum(widths) != block[1]:
        shape = tuple(sizes[d] for d in left) + block
        return [jax.ShapeDtypeStruct(shape, dtype if left else jnp.float32)], widths
    return [jax.ShapeDtypeStruct((block[0], w), jnp.float32) for w in widths], None


def cut_columns(parts, widths):
    if widths is None:
        return parts
    full = parts[0].reshape(-1, sum(widths))
    edges = np.cumsum([0] + list(widths))
    return [full[:, int(lo) : int(hi)] for lo, hi in zip(edges[:-1], edges[1:])]


def reduce_all(grads, orders, sizes, collective_id, spill=None, splits=None, name="reduce"):
    ins, scratch, shapes, counts, all_dims, cuts, later = [], [], [], [], [], [], []
    splits = splits or [None] * len(grads)
    total = 0
    devices = sizes["x"] * sizes["c"] * sizes["z"] * sizes["y"]
    for grad, order, widths in zip(grads, orders, splits):
        dims = SLOTS[-(grad.ndim - 2) :] if grad.ndim > 2 else SLOTS
        if grad.ndim == 2:
            whole = tuple(sizes[d] for d in SLOTS)
            grad = grad.reshape(whole + tile_block(grad.shape[0] // devices, grad.shape[1]))
        block = grad.shape[-2:]
        ins.append(grad)
        all_dims.append(dims)
        more, taken, needed, left = stage_buffers(sizes, block, grad.dtype, dims, order)
        scratch += more
        total += needed
        counts.append(taken)
        ends, widths = cut_shapes(block, left, widths, sizes, grad.dtype)
        shapes += ends
        cuts.append(len(ends))
        later.append(widths)
    if spill is not None:
        ins.append(spill)
        shapes.append(jax.ShapeDtypeStruct(spill.shape, spill.dtype))
        total += 1
    outs = pl.pallas_call(
        functools.partial(reduce_kernel, sizes, orders, all_dims, counts, cuts, int(spill is not None)),
        in_specs=[pl.BlockSpec(memory_space=pltpu.VMEM)] * len(ins),
        out_specs=[pl.BlockSpec(memory_space=pltpu.VMEM)] * len(shapes),
        out_shape=shapes,
        scratch_shapes=scratch + [pltpu.SemaphoreType.DMA((total,)), pltpu.SemaphoreType.DMA((total,))],
        compiler_params=pltpu.CompilerParams(
            collective_id=collective_id, has_side_effects=True, vmem_limit_bytes=56 << 20
        ),
        name=name,
    )(*ins)
    outs = list(outs)
    results = []
    for cut, widths in zip(cuts, later):
        results.append(cut_columns([outs.pop(0) for _ in range(cut)], widths))
    return results + outs


def collect_task(sizes, me, src, out, ybuf, chain, sems, produce):
    z, y, n, fast = me["z"], me["y"], sizes["z"], sizes["y"]
    fan = sems.take((fast - 1) * n)
    base = sems.take(2 * n)

    def fan_copy(k, j):
        to = lax.rem(y + k, fast)
        index = fan + (k - 1) * n + j
        return sems.copy(src.at[j, to], ybuf.at[k - 1, j], index, device_at(sizes, me, "y", to))

    def spread(i, carry):
        far = n - 1 - lax.div(i, 2)
        j = jnp.where(lax.rem(i, 2) == 0, z + far, z - far)

        @pl.when((j >= 0) & (j < n))
        def _():
            produce(j)
            for k in range(1, fast):
                fan_copy(k, j).start()

        return carry

    def chain_copy(side, j, to, plain=False):
        buf = chain.at[side, j]
        return sems.copy(ybuf.at[0, j] if plain else buf, buf, base + side * n + j, device_at(sizes, me, "z", to))

    slots = []
    for slot in range(n - 1):
        for side in range(2):
            lead = z if side == 0 else n - 1 - z
            j = lax.rem((n - 1 - slot + z) if side == 0 else (slot + 1 + z + n), n)
            to = z + 1 if side == 0 else z - 1
            ends = (chain_copy(side, j, to, True), chain_copy(side, j, to))
            slots.append((side, j, ends, lead == 0, (lead > 0) & (lead <= slot), lead <= slot))
    fans = [fan_copy(k, j) for j in range(n) for k in range(1, fast)]
    lax.fori_loop(0, 2 * n - 1, spread, 0)
    yield

    def merge(j):
        for k in range(1, fast):
            fan_copy(k, j).wait_recv()
        value = src[j, y].astype(jnp.float32)
        for k in range(1, fast):
            value = value + ybuf[k - 1, j].astype(jnp.float32)
        return value

    for slot in range(n - 1):
        for side, j, (plain, summed), is_first, is_later, _ in slots[2 * slot : 2 * slot + 2]:

            def begin(plain=plain, j=j):
                ybuf[0, j] = merge(j).astype(ybuf.dtype)
                plain.start()

            def pass_on(summed=summed, side=side, j=j):
                value = merge(j)
                summed.wait_recv()
                chain[side, j] = (chain[side, j].astype(jnp.float32) + value).astype(chain.dtype)
                summed.start()

            pl.when(is_first)(begin)
            pl.when(is_later)(pass_on)
        yield
    out[...] = merge(z)

    def finish(side):
        chain_copy(side, z, z).wait_recv()
        out[...] += chain[side, z].astype(jnp.float32)

    pl.when(z > 0)(partial(finish, 0))
    pl.when(z < n - 1)(partial(finish, 1))
    for fan_end in fans:
        fan_end.wait_send()
    for _, _, (_, summed), _, _, active in slots:
        pl.when(active)(summed.wait_send)


def halve_kernel(sizes, apart, *refs):
    n, count = sizes["x"], len(apart)
    refs = list(refs)
    ins = [refs.pop(0) for _ in range(count)]
    outs = [[refs.pop(0) for _ in range(n)] if alone else refs.pop(0) for alone in apart]
    bufs = [refs.pop(0) for _ in range(count)]
    send_sem, recv_sem = refs
    me = place(sizes)
    greet(sizes, me, ("c",))
    sems = Sems(send_sem, recv_sem)
    c = me["c"]
    peer = device_at(sizes, me, "c", 1 - c)
    sends = {}
    for k in range(n - 1, -1, -1):
        for i, alone in enumerate(apart):
            at = lax.rem(me["x"] + k, n) if alone else k
            sends[k, i] = sems.copy(ins[i].at[at, 1 - c], bufs[i].at[k], sems.take(1), peer)
            sends[k, i].start()
    for k in range(n - 1, -1, -1):
        for i, alone in enumerate(apart):
            at = lax.rem(me["x"] + k, n) if alone else k
            sends[k, i].wait_recv()
            src = ins[i]

            def own(spots, src=src, at=at):
                return src[(at, c) + spots + (slice(None), slice(None))]

            add_pair(outs[i][k] if alone else outs[i].at[k], bufs[i].at[k], own, src.shape[2:-2])
    for send in sends.values():
        send.wait_send()


def halve_cores(grads, apart, sizes, collective_id, name="halve"):
    n = sizes["x"]
    whole = tuple(sizes[d] for d in SLOTS)
    devices = whole[0] * whole[1] * whole[2] * whole[3]
    ins = [g.reshape(whole + tile_block(g.shape[0] // devices, g.shape[1])) for g in grads]
    halves = [g.shape[:1] + g.shape[2:] for g in ins]
    shapes = []
    for h, g, alone in zip(halves, ins, apart):
        shapes += [jax.ShapeDtypeStruct(h[1:], g.dtype)] * n if alone else [jax.ShapeDtypeStruct(h, g.dtype)]
    total = n * len(ins)
    outs = pl.pallas_call(
        functools.partial(halve_kernel, sizes, apart),
        in_specs=[pl.BlockSpec(memory_space=pltpu.VMEM)] * len(ins),
        out_specs=[pl.BlockSpec(memory_space=pltpu.VMEM)] * len(shapes),
        out_shape=shapes,
        scratch_shapes=[pltpu.VMEM(h, g.dtype) for h, g in zip(halves, ins)]
        + [pltpu.SemaphoreType.DMA((total,)), pltpu.SemaphoreType.DMA((total,))],
        compiler_params=pltpu.CompilerParams(
            collective_id=collective_id, has_side_effects=True, vmem_limit_bytes=56 << 20
        ),
        name=name,
    )(*ins)
    outs = list(outs)
    return [[outs.pop(0) for _ in range(n)] if alone else outs.pop(0) for alone in apart]


def feed_forward_kernel(sizes, *refs):
    n = sizes["x"]
    hidden_ref, att_ref, cot_ref, outer_ref, down_ref, gain_ref, inv_ref = refs[:7]
    layer_ref, d_hidden_ref, d_out_ref, scaled_ref, d_gain_ref = refs[7:12]
    wide_outs, down_out = refs[12 : 12 + n], refs[12 + n]
    d_wide, d_down, wide_buf, down_buf, two_ref, low_ref, d_normed, send_sem, recv_sem = refs[13 + n :]
    me = place(sizes)
    greet(sizes, me, ("c",))
    sems = Sems(send_sem, recv_sem)
    c = me["c"]
    peer = device_at(sizes, me, "c", 1 - c)
    width = hidden_ref.shape[1]
    parts = 2 * n
    units = down_ref.shape[0] // parts
    two_ref[...] = hidden_ref[...] + nn_dot(att_ref[...], outer_ref[:, :width])
    gain = gain_ref[...]

    def scale():
        return lax.rsqrt(jnp.mean(two_ref[...] * two_ref[...], axis=1, keepdims=True) + EPSILON)

    low_ref[...] = (two_ref[...] * scale() * gain).astype(jnp.bfloat16)
    d_normed[...] = jnp.zeros_like(d_normed)
    d_hidden_ref[...] = two_ref[...]

    def down_copy(x):
        return sems.copy(d_down.at[x, 1 - c], down_buf.at[x], x, peer)

    def part(i, carry):
        gate_at = pl.ds(pl.multiple_of(i * units, units), units)
        up_at = pl.ds(pl.multiple_of((parts + i) * units, units), units)
        gate_w = outer_ref[:, pl.ds(pl.multiple_of(width + i * units, units), units)]
        up_w = outer_ref[:, pl.ds(pl.multiple_of(width + (parts + i) * units, units), units)]
        down_w = down_ref[gate_at, :]
        low, cot = low_ref[...], cot_ref[...]
        gate, up = nn_dot(low, gate_w), nn_dot(low, up_w)
        square = gate * gate
        bend = jnp.tanh(0.7978845608 * gate * (1.0 + 0.044715 * square))
        half = 0.5 * (1.0 + bend)
        act = gate * half
        slope = half + gate * (0.5 * (1.0 - bend * bend)) * (0.7978845608 * (1.0 + 3.0 * 0.044715 * square))
        inner = (act * up).astype(jnp.bfloat16)
        d_hidden_ref[...] += nn_dot(inner, down_w)
        d_inner = nt_dot(cot, down_w)
        d_gate = (d_inner * up * slope).astype(jnp.bfloat16)
        d_up = (d_inner * act).astype(jnp.bfloat16)
        d_down[lax.div(i, 2), lax.rem(i, 2)] = (
            tn_dot(inner, cot).astype(jnp.bfloat16).reshape(d_down.shape[2:])
        )
        pl.when(lax.rem(i, 2) != c)(lambda: down_copy(lax.div(i, 2)).start())
        block = d_wide.shape[:-1] + (units,)
        d_wide[..., gate_at] = tn_dot(low, d_gate).astype(jnp.bfloat16).reshape(block)
        d_wide[..., up_at] = tn_dot(low, d_up).astype(jnp.bfloat16).reshape(block)
        d_normed[...] += nt_dot(d_gate, gate_w) + nt_dot(d_up, up_w)
        return carry

    lax.fori_loop(0, parts, part, 0)
    sends = [down_copy(x) for x in range(n)]
    for x in range(n):
        send = sems.copy(d_wide.at[x, 1 - c], wide_buf.at[x], n + x, peer)
        send.start()
        sends.append(send)
    layer_ref[...] = d_hidden_ref[...].astype(jnp.bfloat16)
    two, s2 = two_ref[...], scale()
    pulled = gain * d_normed[...]
    d_gain_ref[...] = jnp.sum(d_normed[...] * two * s2, axis=0, keepdims=True)
    drift = jnp.mean(two * pulled, axis=1, keepdims=True)
    d_two = cot_ref[...].astype(jnp.float32) + s2 * pulled - two * (s2 * s2 * s2 * drift)
    d_hidden_ref[...] = d_two
    d_low = d_two.astype(jnp.bfloat16)
    d_out_ref[...] = tn_dot(att_ref[...], d_low).astype(jnp.bfloat16)
    d_att = nt_dot(d_low, outer_ref[:, :width]).astype(jnp.bfloat16)
    scaled_ref[...] = (d_att.astype(jnp.float32) * inv_ref[...]).astype(jnp.bfloat16)
    for send in sends:
        send.wait_recv()
    for x in range(n):
        add_pair(down_out.at[x], down_buf.at[x], lambda at, x=x: d_down[(x, c) + at], d_down.shape[2:-2])
        at_x = lax.rem(me["x"] + x, n)
        add_pair(wide_outs[x], wide_buf.at[at_x], lambda at, at_x=at_x: d_wide[(at_x, c) + at], d_wide.shape[2:-2])
    for send in sends:
        send.wait_send()


def feed_forward(hidden_one, attended, cotangent, outer_w, down_w, gain, inverse, sizes, collective_id):
    n = sizes["x"]
    whole = tuple(sizes[d] for d in SLOTS)
    devices = whole[0] * whole[1] * whole[2] * whole[3]
    count, width = hidden_one.shape
    hidden = down_w.shape[0]
    bf16, f32 = jnp.bfloat16, jnp.float32
    wide_block = (width // devices, 2 * hidden)
    down_block = (hidden // devices, width)
    plane = whole[2:]
    vmem = pl.BlockSpec(memory_space=pltpu.VMEM)
    outs = pl.pallas_call(
        functools.partial(feed_forward_kernel, sizes),
        in_specs=[vmem] * 7,
        out_specs=[vmem] * (6 + n),
        out_shape=[
            jax.ShapeDtypeStruct((count, width), bf16),
            jax.ShapeDtypeStruct((count, width), f32),
            jax.ShapeDtypeStruct((width, width), bf16),
            jax.ShapeDtypeStruct((count, width), bf16),
            jax.ShapeDtypeStruct((1, width), f32),
        ]
        + [jax.ShapeDtypeStruct(plane + wide_block, bf16)] * n
        + [jax.ShapeDtypeStruct((n,) + plane + down_block, bf16)],
        scratch_shapes=[
            pltpu.VMEM(whole + wide_block, bf16),
            pltpu.VMEM(whole + down_block, bf16),
            pltpu.VMEM((n,) + plane + wide_block, bf16),
            pltpu.VMEM((n,) + plane + down_block, bf16),
            pltpu.VMEM((count, width), f32),
            pltpu.VMEM((count, width), bf16),
            pltpu.VMEM((count, width), f32),
            pltpu.SemaphoreType.DMA((2 * n,)),
            pltpu.SemaphoreType.DMA((2 * n,)),
        ],
        compiler_params=pltpu.CompilerParams(
            collective_id=collective_id, has_side_effects=True, vmem_limit_bytes=60 << 20
        ),
        name="feed_forward",
    )(hidden_one, attended, cotangent, outer_w, down_w, gain, inverse)
    return list(outs[:5]) + [list(outs[5 : 5 + n]), outs[5 + n]]


def from_others(pieces, sizes):
    n = sizes["x"]
    got = []
    for k in range(1, n):
        pairs = [(((x + k) % n) * 2 + c, x * 2 + c) for x in range(n) for c in range(2)]
        got.append(lax.ppermute(pieces[n - k], "batch", pairs))
    return got


def back_rows_kernel(sizes, rows, tasks_info, inner, *refs):
    refs = list(refs)

    def take(count):
        taken = refs[:count]
        del refs[:count]
        return taken

    info_ref, far_ref, diag_ref, q_ref, g_ref, full_ref, peak_ref, kv_ref, dkv_ref, normed_ref, second_ref = take(11)
    if inner:
        own_ref, dq_before_ref, d_out_ref = take(3)
    grads = [take(info[4]) for info in tasks_info]
    d_normed_ref, dq_ref, near_ref = take(3)
    outs = [take(info[3]) for info in tasks_info]
    last_ref = take(1)[0]
    if inner:
        inner_ref = take(1)[0]
        inner_counts = inner
        d_last_ref = take(1)[0]
    else:
        d_last_ref = last_ref
    kv_buf, chunk_ref, normed_buf, d_rows_ref, ybuf, chain, bias_ref, sum_ref, acc_ref, total_ref = take(10)
    kv_sem, chunk_sem, normed_sem, send_sem, recv_sem = refs[-5:]
    bufs = refs[:-5]
    me = place(sizes)
    first = me["z"] * sizes["y"] + me["y"]
    seqs, length, _ = kv_ref.shape
    n = sizes["z"]
    step = length // n
    last = seqs - 1
    width = q_ref.shape[1]
    pairs = diag_ref.shape[0]
    wide = width // pairs
    fetch = pltpu.make_async_copy(kv_ref.at[last], kv_buf, kv_sem)
    fetch.start()
    greet(sizes, me, SLOTS + ("s",))
    sems = Sems(send_sem, recv_sem)
    ffn = []
    for (order, dims, counts, _, many), grad, out in zip(tasks_info, grads, outs):
        src = grad[0]
        if many > 1:
            src = bufs.pop(0)

            def total(spots, src=src, grad=grad):
                here = spots + (slice(None), slice(None))
                value = grad[0][here].astype(jnp.float32)
                for more in grad[1:]:
                    value = value + more[here].astype(jnp.float32)
                src[here] = value.astype(src.dtype)

            over(src.shape[:-2], total)
        stages = stage_refs(sizes, order, counts, bufs)
        ffn.append(reduce_task(sizes, me, src, out[0] if len(out) == 1 else Split(out), stages, sems, order, dims))
        next(ffn[-1])
    wide_task, down_task = ffn

    def rows_of(p):
        def produce(j):
            here = pl.ds(pl.multiple_of(j * step, step), step)
            if p < last:
                copy = pltpu.make_async_copy(dkv_ref.at[p, here], chunk_ref.at[0], chunk_sem.at[0])
                copy.start()
                copy.wait()
                block = chunk_ref[0]
            else:
                block = d_last_ref[here, :]
            block = nt_dot(block, second_ref[...]).astype(jnp.bfloat16)
            d_rows_ref[p, j] = block.reshape(d_rows_ref.shape[2:])

        return collect_task(
            sizes, me, d_rows_ref.at[p], d_normed_ref.at[p], ybuf.at[p], chain.at[p], sems, produce
        )

    before = [rows_of(p) for p in range(last)]
    for task in before:
        next(task)
    fetch.wait()
    size = info_ref[last]

    def one_pair(p, carry):
        fill_bias(rows, far_ref, diag_ref.at[pl.ds(p, 1)], bias_ref, p)
        sum_ref[...] = jnp.zeros_like(sum_ref)
        lanes = pl.ds(pl.multiple_of(p * wide, wide), wide)
        tail = slice(last * rows, seqs * rows)
        k_lanes = pl.ds(pl.multiple_of(2 * p * wide, wide), wide)
        v_lanes = pl.ds(pl.multiple_of((2 * p + 1) * wide, wide), wide)

        def write(here, dk, dv):
            d_last_ref[here, k_lanes] = dk
            d_last_ref[here, v_lanes] = dv

        dq_ref[:, lanes] = back_pair(
            rows,
            size,
            first,
            q_ref[tail, lanes],
            g_ref[tail, lanes],
            full_ref[tail, lanes],
            (lambda here: (kv_buf[here, k_lanes], kv_buf[here, v_lanes]), length // (SPAN * rows)),
            [peak_ref[last, p, a : a + 1, :] for a in range(2)],
            bias_ref,
            sum_ref,
            acc_ref,
            write,
        )

        def keep(a, slot, value):
            near_ref[p, a, slot] = value

        near_sums(rows, sum_ref, keep)
        for i in range(min(pairs, n - 1)):

            @pl.when(p == i)
            def _():
                for task in before:
                    next(task, None)

        @pl.when(p == pairs - 1)
        def _():
            next(wide_task)
            next(down_task)

        return carry

    lax.fori_loop(0, pairs, one_pair, 0)
    after = rows_of(last)
    next(after)
    tasks = ffn + before + [after]
    if inner:
        steps = seqs * n
        early = last * n

        def at_step(i):
            return pl.ds(pl.multiple_of(i * step, step), step)

        def normed_copy(i):
            slot = lax.rem(i, 2)
            return pltpu.make_async_copy(normed_ref.at[at_step(i)], normed_buf.at[slot], normed_sem.at[slot])

        def early_copy(i):
            slot = lax.rem(i, 2)
            src = dkv_ref.at[lax.div(i, n), at_step(lax.rem(i, n))]
            return pltpu.make_async_copy(src, chunk_ref.at[slot], chunk_sem.at[slot])

        normed_copy(0).start()
        early_copy(0).start()
        total_ref[...] = jnp.zeros_like(total_ref)

        plan = [[], before, [], [wide_task], [after], [], [after]]

        def weigh(i, carry):
            pl.when(i + 1 < steps)(lambda: normed_copy(i + 1).start())
            pl.when(i + 1 < early)(lambda: early_copy(i + 1).start())
            normed_copy(i).wait()
            slot = lax.rem(i, 2)

            @pl.when(i < early)
            def _():
                early_copy(i).wait()
                total_ref[...] += tn_dot(normed_buf[slot], chunk_ref[slot])

            @pl.when(i >= early)
            def _():
                total_ref[...] += tn_dot(normed_buf[slot], d_last_ref[at_step(i - early), :])

            for k, tasks_now in enumerate(plan):

                @pl.when(i == k)
                def _():
                    for task in tasks_now:
                        next(task, None)

            return carry

        lax.fori_loop(0, steps, weigh, 0)
        block = inner_ref.shape[:-1]
        d_query = tn_dot(own_ref[last * rows :], dq_ref[...])
        if last:
            d_query = d_query + tn_dot(own_ref[: last * rows], dq_before_ref[...])
        inner_ref[..., :width] = d_query.astype(jnp.bfloat16).reshape(block + (width,))
        inner_ref[..., width : 2 * width] = d_out_ref[...]
        inner_ref[..., 2 * width :] = total_ref[...].astype(jnp.bfloat16).reshape(block + (2 * width,))
        stages = stage_refs(sizes, "cx", inner_counts, bufs)
        tasks.insert(0, reduce_task(sizes, me, inner_ref, last_ref, stages, sems, "cx", SLOTS))
    run_together(tasks)


def back_rows(info, far, diag, q, g, full, kv, peak, dkv, normed_all, normed_own, second, dq_before, d_out, grads,
              orders, splits, sizes, rows, collective_id, name="back_rows"):
    seqs, length, double = kv.shape
    width = q.shape[1]
    last = seqs - 1
    pairs = far.shape[0] // 2
    n, fast = sizes["z"], sizes["y"]
    step = length // n
    smem, vmem = pl.BlockSpec(memory_space=pltpu.SMEM), pl.BlockSpec(memory_space=pltpu.VMEM)
    anywhere = pl.BlockSpec(memory_space=pl.ANY)
    bf16, f32 = jnp.bfloat16, jnp.float32
    ins = [info, far, diag, q, g, full, peak, kv, dkv, normed_all, second]
    in_specs = [smem, smem] + [vmem] * 5 + [anywhere] * 3 + [vmem]
    devices = sizes["x"] * sizes["c"] * n * fast
    own_block = (width // devices, 4 * width)
    inner = None
    scratch, total = [], 0
    if own_block[0] % 16 == 0:
        whole = tuple(sizes[d] for d in SLOTS)
        more, inner, needed, left = stage_buffers(sizes, own_block, bf16, SLOTS, "cx")
        inner_more = more
        total += needed
        ins += [normed_own, dq_before, d_out.reshape(whole + (own_block[0], width))]
        in_specs += [vmem] * 3
        last_shape = jax.ShapeDtypeStruct(tuple(sizes[d] for d in left) + own_block, bf16)
    else:
        last_shape = jax.ShapeDtypeStruct((length, double), bf16)
    tasks_info, shapes, later = [], [], []
    for grad, order, widths in zip(grads, orders, splits):
        many = isinstance(grad, list)
        given = grad if many else [grad]
        block = given[0].shape[-2:]
        dims = ("z", "y") if many else ("x", "z", "y")
        more, counts, needed, left = stage_buffers(sizes, block, given[0].dtype, dims, order)
        if len(given) > 1:
            more = [pltpu.VMEM(given[0].shape, given[0].dtype)] + more
        scratch += more
        total += needed
        ends, widths = cut_shapes(block, left, widths, sizes, given[0].dtype)
        shapes += ends
        later.append(widths)
        tasks_info.append((order, dims, counts, len(ends), len(given)))
        ins += given
        in_specs += [vmem] * len(given)
    head_shapes = [
        jax.ShapeDtypeStruct((seqs, rows, width), f32),
        jax.ShapeDtypeStruct((rows, width), bf16),
        jax.ShapeDtypeStruct((pairs, 2, 5, 8, 2 * rows), f32),
    ]
    own_scratch = []
    if inner:
        own_scratch = [pltpu.VMEM(whole + own_block, bf16), pltpu.VMEM((length, double), bf16)]
        scratch = scratch + inner_more
    block = (seqs, n, fast, rows, width)
    own_scratch += [
        pltpu.VMEM((length, double), bf16),
        pltpu.VMEM((2, step, double), bf16),
        pltpu.VMEM((2, step, width), bf16),
        pltpu.VMEM(block, bf16),
        pltpu.VMEM((seqs, fast - 1, n, rows, width), bf16),
        pltpu.VMEM((seqs, 2, n, rows, width), bf16),
        pltpu.VMEM((2, 5, rows, rows), f32),
        pltpu.VMEM((2, 5, rows, rows), f32),
        pltpu.VMEM((2, width // pairs, rows), f32),
        pltpu.VMEM((width, double), f32) if inner else pltpu.VMEM((8, 128), f32),
    ]
    total += seqs * ((fast - 1) * n + 2 * n)
    outs = pl.pallas_call(
        functools.partial(back_rows_kernel, sizes, rows, tasks_info, inner),
        in_specs=in_specs,
        out_specs=[vmem] * (len(shapes) + 4),
        out_shape=head_shapes + shapes + [last_shape],
        scratch_shapes=own_scratch
        + scratch
        + [
            pltpu.SemaphoreType.DMA,
            pltpu.SemaphoreType.DMA((2,)),
            pltpu.SemaphoreType.DMA((2,)),
            pltpu.SemaphoreType.DMA((total,)),
            pltpu.SemaphoreType.DMA((total,)),
        ],
        compiler_params=pltpu.CompilerParams(
            collective_id=collective_id, has_side_effects=True, vmem_limit_bytes=62 << 20
        ),
        name=name,
    )(*ins)
    outs = list(outs)
    heads = [outs.pop(0) for _ in range(3)]
    results = []
    for (_, _, _, cut, _), widths in zip(tasks_info, later):
        results.append(cut_columns([outs.pop(0) for _ in range(cut)], widths))
    return heads + results + [outs[0], inner is not None]


def on_device(
    inputs,
    lengths,
    conv_taps,
    gain_attn,
    w_proj,
    w_query,
    w_key,
    w_value,
    w_out,
    gain_ffn,
    w_gate,
    w_up,
    w_down,
    rel_bias,
    cotangent,
):
    batch, seq = lax.axis_size("batch"), lax.axis_size("seq")
    sizes = layout_of(batch, seq)
    devices = batch * seq
    seqs, rows, width = inputs.shape
    length = rows * seq
    count = seqs * rows
    own = w_proj.shape[0]
    own_bias = rel_bias.shape[0]
    heads = own_bias * devices // NB
    hidden = w_gate.shape[1]

    small = jnp.concatenate(
        [
            conv_taps,
            gain_attn[:, None],
            gain_ffn[:, None],
            jnp.pad(rel_bias, (0, own - own_bias))[:, None],
            jnp.zeros((own, PACK - TAPS - 3), jnp.bfloat16),
        ],
        axis=1,
    )
    pairs = heads // 2
    key_value_w = jnp.stack([w_key.reshape(own, pairs, -1), w_value.reshape(own, pairs, -1)], axis=2)
    first, second, outer_plane, down_plane, left_rim = gather_all(
        [
            jnp.concatenate([small, w_proj, w_query], axis=1),
            key_value_w.reshape(own, -1),
            jnp.concatenate([w_out, w_gate, w_up], axis=1),
            w_down,
        ],
        ["Zyxc", "Zxyc", "zy", "yz"],
        sizes,
        1,
        rim=inputs[:, rows - 16 :, :],
        name="gather_first",
    )
    first = first.reshape(width, -1)
    second = second.reshape(width, -1)
    taps = first[:, :TAPS].astype(jnp.float32)
    gain_first = first[:, TAPS].astype(jnp.float32)
    gain_second = first[:, TAPS + 1].astype(jnp.float32)
    table = first[:, TAPS + 2].reshape(devices, own)[:, :own_bias].reshape(heads, NB).astype(jnp.float32)
    proj_w = first[:, PACK : PACK + width]
    query_w = first[:, PACK + width :]

    padded = jnp.concatenate([left_rim[:, 13:], inputs], axis=1).astype(jnp.float32)
    mixed_conv, conv_back = jax.vjp(partial(conv_mix, row_count=rows), padded, taps)
    mixed_low = mixed_conv.astype(jnp.bfloat16).reshape(count, width)
    resid_in = inputs.astype(jnp.float32).reshape(count, width)
    hidden_one = resid_in + mat_dot(mixed_low, proj_w)
    normed_one, norm_one_back = jax.vjp(norm_rows, hidden_one, gain_first)
    normed_low = normed_one.astype(jnp.bfloat16)

    outer_w, down_w, normed_all = gather_all(
        [outer_plane, down_plane],
        ["xc", "xc"],
        sizes,
        2,
        rows=normed_low.reshape(seqs, rows, width),
        plan=(0, 1, 2, 2, 2, 2),
        name="gather_rows",
    )
    outer_w = outer_w.reshape(width, -1)
    down_w = down_w.reshape(hidden, -1)
    out_w = outer_w[:, :width]
    wide_w = outer_w[:, width:]
    normed_all = normed_all.reshape(seqs * length, width)
    queries = mat_dot(normed_low, query_w).astype(jnp.bfloat16)
    key_value = mat_dot(normed_all, second).astype(jnp.bfloat16).reshape(seqs, length, 2 * width)

    far, diag = bias_tables(table, rows)
    info = jnp.concatenate([lengths, lax.axis_index("seq")[None].astype(jnp.int32)])
    attended, attended_full, inverse, peak = attend(info, far, diag, queries, key_value, rows, length)

    grad_low = cotangent.reshape(count, width)
    if own % 16 == 0:
        layer_out, d_hidden_two, d_out_w, scaled, d_gain_two, wide_pieces, down_half = feed_forward(
            hidden_one, attended, grad_low, outer_w, down_w, gain_second[None], inverse, sizes, 4
        )
        d_gain_two = d_gain_two[0]
    else:
        hidden_two = hidden_one + mat_dot(attended, out_w)
        normed_two, norm_two_back = jax.vjp(norm_rows, hidden_two, gain_second)
        normed_two_low = normed_two.astype(jnp.bfloat16)
        both_pre = mat_dot(normed_two_low, wide_w)
        inner_act, inner_back = jax.vjp(gated, both_pre[:, :hidden], both_pre[:, hidden:])
        inner_low = inner_act.astype(jnp.bfloat16)
        layer_out = (hidden_two + mat_dot(inner_low, down_w)).astype(jnp.bfloat16)

        d_down_w = outer_sum(inner_low, grad_low).astype(jnp.bfloat16)
        d_gate, d_up = inner_back(back_dot(grad_low, down_w))
        d_both = jnp.concatenate([d_gate.astype(jnp.bfloat16), d_up.astype(jnp.bfloat16)], axis=1)
        d_wide_w = outer_sum(normed_two_low, d_both).astype(jnp.bfloat16)
        d_hidden_part, d_gain_two = norm_two_back(back_dot(d_both, wide_w))
        d_hidden_two = grad_low.astype(jnp.float32) + d_hidden_part
        d_attn_low = d_hidden_two.astype(jnp.bfloat16)
        d_out_w = outer_sum(attended, d_attn_low).astype(jnp.bfloat16)
        d_attended = back_dot(d_attn_low, out_w).astype(jnp.bfloat16)
        scaled = (d_attended.astype(jnp.float32) * inverse).astype(jnp.bfloat16)
        wide_pieces, down_half = halve_cores([d_wide_w, d_down_w], [True, False], sizes, 4)
    scaled, wide_pieces, down_half, d_out_w, layer_out = lax.optimization_barrier(
        (scaled, wide_pieces, down_half, d_out_w, layer_out)
    )
    wide_others = from_others(wide_pieces, sizes)
    early = seqs - 1
    dq_before, dkv_before, near_before = attend_back(
        info, far, diag, queries, scaled, attended_full, key_value, peak, rows, length, early
    )
    dq_before, dkv_before, near_before, wide_others = lax.optimization_barrier(
        (dq_before, dkv_before, near_before, wide_others)
    )
    d_normed_one, dq_last, near, (g_gate, g_up), (g_down,), last, joined = back_rows(
        info,
        far,
        diag,
        queries,
        scaled,
        attended_full,
        key_value,
        peak,
        dkv_before,
        normed_all,
        normed_low,
        second,
        dq_before,
        d_out_w,
        [[wide_pieces[0]] + wide_others, down_half],
        ["Zy", "xs"],
        [(hidden, hidden), None],
        sizes,
        rows,
        5,
    )
    d_table = bias_grad(near_before + near, rows).reshape(heads * NB)
    d_queries = jnp.concatenate([dq_before, dq_last], axis=0)
    if joined:
        inner, inner_order = last, "s"
    else:
        d_key_value = jnp.concatenate([dkv_before, last[None]], axis=0).reshape(seqs * length, 2 * width)
        d_second_w = outer_sum(normed_all, d_key_value).astype(jnp.bfloat16)
        d_query_w = outer_sum(normed_low, d_queries).astype(jnp.bfloat16)
        inner, inner_order = jnp.concatenate([d_query_w, d_out_w, d_second_w], axis=1), "cxs"
    d_normed_one = d_normed_one.reshape(count, width)
    d_normed_one = d_normed_one + back_dot(d_queries, query_w)
    d_first_part, d_gain_one = norm_one_back(d_normed_one)
    d_hidden_one = d_hidden_two + d_first_part
    d_mix_low = d_hidden_one.astype(jnp.bfloat16)
    d_proj_w = outer_sum(mixed_low, d_mix_low).astype(jnp.bfloat16)
    d_mixed = back_dot(d_mix_low, proj_w).reshape(seqs, rows, width)
    d_padded, d_taps = conv_back(d_mixed)
    d_inputs = d_hidden_one.reshape(seqs, rows, width) + d_padded[:, 3:, :]
    d_small = jnp.concatenate(
        [
            d_taps.T,
            d_gain_one[None],
            d_gain_two[None],
            jnp.pad(d_table.reshape(devices, own_bias), ((0, 0), (0, own - own_bias))).reshape(1, width),
            jnp.zeros((16 - TAPS - 3, width), jnp.float32),
        ],
        axis=0,
    )
    d_last = jnp.concatenate([d_proj_w, jnp.pad(d_small.T, ((0, 0), (0, PACK - 16))).astype(jnp.bfloat16)], axis=1)
    (g_proj, g_small), (g_query, g_out, g_second), spill = reduce_all(
        [d_last, inner],
        ["cxs", inner_order],
        sizes,
        6,
        spill=d_padded[:, :8, :],
        splits=[(width, PACK), (width, width, 2 * width)],
    )
    input_grad = d_inputs.at[:, rows - 3 :, :].add(spill[:, :3]).astype(jnp.bfloat16)
    g_second = g_second.reshape(own, pairs, 2, -1)
    return (
        layer_out.reshape(seqs, rows, width),
        input_grad,
        g_small[:, :TAPS],
        g_small[:, TAPS],
        g_proj,
        g_query,
        g_second[:, :, 0].reshape(own, width),
        g_second[:, :, 1].reshape(own, width),
        g_out,
        g_small[:, TAPS + 1],
        g_gate,
        g_up,
        g_down.reshape(w_down.shape),
        g_small[:own_bias, TAPS + 2],
    )


def solution(mesh):
    in_specs = (
        P("batch", "seq", None),
        P("batch"),
        P(("batch", "seq"), None),
        P(("batch", "seq")),
        P(("batch", "seq"), None),
        P(("batch", "seq"), None),
        P(("batch", "seq"), None),
        P(("batch", "seq"), None),
        P(("batch", "seq"), None),
        P(("batch", "seq")),
        P(("batch", "seq"), None),
        P(("batch", "seq"), None),
        P(("batch", "seq"), None),
        P(("batch", "seq")),
        P("batch", "seq", None),
    )
    out_specs = (
        P("batch", "seq", None),
        P("batch", "seq", None),
        P(("batch", "seq"), None),
        P(("batch", "seq")),
        P(("batch", "seq"), None),
        P(("batch", "seq"), None),
        P(("batch", "seq"), None),
        P(("batch", "seq"), None),
        P(("batch", "seq"), None),
        P(("batch", "seq")),
        P(("batch", "seq"), None),
        P(("batch", "seq"), None),
        P(("batch", "seq"), None),
        P(("batch", "seq")),
    )
    return jax.shard_map(
        on_device, mesh=mesh, in_specs=in_specs, out_specs=out_specs, check_vma=False
    )
```

profile of v0, /device:TPU:0, one launch (start us, length us, event | category | flops | bytes accessed | tf_op | source)
XLA Modules:
  0.0 331.2 jit_solution(6244467103525178718)
XLA Ops:
  0.7 0.8 stack_reshape.8
  1.4 0.7 stack_reshape.9
  2.3 0.6 reshape.271.refs_1_
  2.9 0.7 pad_bitcast_fusion
  3.7 0.7 copy.64
  4.4 0.7 copy.65
  5.2 1.4 slice.171.refs_4_
  6.5 1.5 pad_maximum_fusion.refs_2_
  8.1 1.5 concatenate.28.refs_0_
  9.5 42.1 %gather_first.1 = (bf16[2,2,4,2,16,1152]{5,4,3,2,1,0:T(8,128)(2,1)}, bf16[2,2,4,2,16,1024]{5,4,3,2,1,0:T(8,128)(2,1)}, bf16[4,2,16,4608]{3,2,1,0:T(8,128)(2,1)},...) custom-call(bf16[16,1152]{1,0:T(8,128)(2,1)} %concatenate.28.refs_0_, bf16[16,1024]{1,0:T(8,128)(2,1)} %reshape.271.refs_1_, ...), custom_call_target="tpu_custom_call" | custom-call | tf_op jit(solution)/shard_map/gather_first/pallas_call | solution.py:623
  51.7 0.9 slice.210
  52.6 1.3 fusion.39
  54.0 0.7 slice.174
  54.9 3.1 add_convert_fusion
  58.0 0.5 multiply_reduce_fusion.11
  58.5 0.3 copy-done.16
  58.9 0.9 copy-done.13
  60.0 0.4 convolution_convert_fusion.2.q_ref.refs_3_
  61.0 0.6 bitcast_convert_fusion.refs_5_
  61.6 53.9 %gather_rows.1 = (bf16[2,2,4,2,16,4608]{5,4,3,2,1,0:T(8,128)(2,1)}, bf16[2,2,4,2,64,512]{5,4,3,2,1,0:T(8,128)(2,1)}, bf16[2,4,2,256,512]{4,3,2,1,0:T(8,128)(2,1)}) custom-call(bf16[4,2,16,4608]{3,2,1,0:T(8,128)(2,1)} %get-tuple-element.98.refs_0_, bf16[4,2,64,512]{3,2,1,0:T(8,128)(2,1)} %get-tuple-element.99.refs_1_, bf16[2,256,512]{2,1,0:T(8,128)(2,1)} %bitcast.73), custom_call_target="tpu_custom_call" | custom-call | tf_op jit(solution)/shard_map/gather_rows/pallas_call | solution.py:623
  115.6 9.2 %convolution_convert_fusion = bf16[4096,1024]{1,0:T(8,128)(2,1)} fusion(bf16[4096,512]{1,0:T(8,128)(2,1)} %bitcast.77, bf16[512,1024]{1,0:T(8,128)(2,1)S(1)} %bitcast.91), kind=kOutput, calls=%fused_computation.1 | convolution fusion | flops 4299161600 | bytes 13631488 | tf_op jit(solution)/shard_map/dot_general | solution.py:21
  124.9 19.2 %attend.1 = (bf16[512,512]{1,0:T(8,128)(2,1)S(1)}, f32[512,512]{1,0:T(8,128)S(1)}, f32[512,512]{1,0:T(8,128)S(1)}, f32[2,4,2,256]{3,2,1,0:T(2,128)S(1)}) custom-call(s32[3]{0:T(128)S(1)} %pad_add_fusion.1.info_ref.refs_0_, f32[8,2]{1,0:T(8,128)S(1)} %pad_maximum_fusion.2.far_ref.refs_1_, f32[4,6,512]{2,1,0:T(8,128)S(1)} %reshape.275.diag_ref.refs_2_, ...), custom_call_target="tpu_custom_call" | custom-call | flops 8589934592 | bytes 17825792 | tf_op jit(solution)/shard_map/attend/pallas_call | solution.py:191
  144.1 1.0 copy-done.3
  145.1 0.8 copy-done.6
  145.9 24.2 %feed_forward.1 = (bf16[512,512]{1,0:T(8,128)(2,1)}, f32[512,512]{1,0:T(8,128)}, bf16[512,512]{1,0:T(8,128)(2,1)}, bf16[512,512]{1,0:T(8,128)(2,1)}, f32[1,512]{...) custom-call(f32[512,512]{1,0:T(8,128)} %copy-done.13, ...), custom_call_target="tpu_custom_call" | custom-call | tf_op jit(solution)/shard_map/feed_forward/pallas_call | solution.py:1167
  170.1 2.0 collective-permute-start
  172.1 0.6 compare_reduce_fusion
  172.7 1.0 iota_compare_fusion
  173.7 0.7 convert.28
  174.4 1.0 copy-done.5
  175.4 19.5 %attend_back.1 = (bf16[256,512]{1,0:T(8,128)(2,1)S(1)}, bf16[1,2048,1024]{2,1,0:T(8,128)(2,1)}, f32[4,2,5,8,512]{4,3,2,1,0:T(8,128)S(1)}) custom-call(s32[3]{0:T(128)S(1)} %pad_add_fusion.1.info_ref.refs_0_, f32[8,2]{1,0:T(8,128)S(1)} %pad_maximum_fusion.2.far_ref.refs_1_, f32[4,6,512]{2,1,0:T(8,128)S(1)} %reshape.275.diag_ref.refs_2_, ...), custom_call_target="tpu_custom_call" | custom-call | flops 12884901888 | bytes 26738688 | tf_op jit(solution)/shard_map/attend_back/pallas_call | solution.py:323
  194.9 0.7 copy-done
  195.7 75.8 %back_rows.1 = (f32[2,256,512]{2,1,0:T(8,128)}, bf16[256,512]{1,0:T(8,128)(2,1)}, f32[4,2,5,8,512]{4,3,2,1,0:T(8,128)}, f32[16,2048]{1,0:T(8,128)}, f32[16,2048]...) custom-call(s32[3]{0:T(128)} %copy-done.10, f32[8,2]{1,0:T(8,128)} %copy-done.9, ...), custom_call_target="tpu_custom_call" | custom-call | tf_op jit(solution)/shard_map/back_rows/pallas_call | solution.py:1462
  271.5 1.3 add.212
  272.9 0.8 slice.232
  273.8 2.0 multiply_reduce_fusion
  275.9 0.3 fusion.19
  276.1 1.5 fusion.26
  277.6 1.3 convolution_convert_fusion.1
  279.1 2.6 select_reduce_fusion
  281.7 0.7 add_select_fusion
  282.9 5.3 %multiply_reduce_fusion.9 = (f32[512]{0:T(512)S(1)}, f32[512]{0:T(512)S(1)}, f32[512]{0:T(512)S(1)}, f32[512]{0:T(512)S(1)}, f32[512]{0:T(512)S(1)}, /*index=5*/...) fusion(f32[2,259,512]{2,1,0:T(8,128)S(1)} %copy-done.12, ...), kind=kLoop, calls=%fused_computation.46 | loop fusion | flops 20442624 | bytes 10508288 | tf_op jit(solution)/shard_map/transpose(jvp())/reduce_sum | solution.py:63
  288.3 1.2 fusion.20
  289.5 1.1 copy.75
  290.9 1.0 copy-done.20
  291.8 0.3 copy-done.21
  292.1 0.9 broadcast_multiply_fusion
  293.1 1.2 pad_add_fusion
  294.3 0.6 slice.235.refs_2_
  294.9 24.4 %reduce.31 = (f32[16,512]{1,0:T(8,128)}, f32[16,128]{1,0:T(8,128)}, f32[16,512]{1,0:T(8,128)}, f32[16,512]{1,0:T(8,128)}, f32[16,1024]{1,0:T(8,128)}, /*index=5*/f32[2,8,512]{2,1,0:T(8,128)}) custom-call(bf16[2,2,4,2,16,640]{5,4,3,2,1,0:T(8,128)(2,1)} %bitcast.85, bf16[4,2,16,2048]{3,2,1,0:T(8,128)(2,1)} %get-tuple-element.132.refs_1_, ...), custom_call_target="tpu_custom_call" | custom-call | tf_op jit(solution)/shard_map/reduce/pallas_call | solution.py:922
  319.3 1.5 slice_reduce_fusion.5
  320.8 1.4 slice_reduce_fusion.7
  322.4 0.5 copy-done.38
  323.1 0.9 convert_element_type.133
  324.3 0.6 copy.86
  324.9 0.6 copy.87
  325.5 0.8 copy.99
  326.3 0.6 copy.100
  326.9 0.6 copy.101
  327.5 0.6 copy.102
  328.1 0.6 copy.103
  328.8 0.7 copy.104
  329.4 0.7 copy.105
  330.1 0.7 copy.106
  (112 shorter events, 3.4 us)
Async XLA Ops:
  0.6 54.1 %copy-start.24 = (bf16[2,256,512]{2,1,0:T(8,128)(2,1)S(1)}, bf16[2,256,512]{2,1,0:T(8,128)(2,1)}, u32[]{:S(2)}) copy-start(bf16[2,256,512]{2,1,0:T(8,128)(2,1)} %param.23) | copy-start | bytes 1572868
  54.9 3.1 copy-start.11
  54.9 3.1 copy-start.22
  58.0 0.8 copy-start.16
  58.8 1.0 copy-start.13
  59.9 1.6 copy-start.15
  60.0 0.7 copy-start.39
  60.4 113.9 %copy-start.4 = (bf16[512,512]{1,0:T(8,128)(2,1)}, bf16[512,512]{1,0:T(8,128)(2,1)S(1)}, u32[]{:S(2)}) copy-start(bf16[512,512]{1,0:T(8,128)(2,1)S(1)} %convolution_convert_fusion.2.q_ref.refs_3_) | copy-start | bytes 1572868
  60.8 113.5 %copy-start.7 = (f32[4,6,512]{2,1,0:T(8,128)}, f32[4,6,512]{2,1,0:T(8,128)S(1)}, u32[]{:S(2)}) copy-start(f32[4,6,512]{2,1,0:T(8,128)S(1)} %reshape.275.diag_ref.refs_2_) | copy-start | bytes 147460
  60.9 54.7 %copy-start.25 = (bf16[2,2,4,2,16,1024]{5,4,3,2,1,0:T(8,128)(2,1)S(1)}, bf16[2,2,4,2,16,1024]{5,4,3,2,1,0:T(8,128)(2,1)}, u32[]{:S(2)}) copy-start(bf16[2,2,4,2,16,1024]{5,4,3,2,1,0:T(8,128)(2,1)} %get-tuple-element.101) | copy-start | bytes 3145732
  115.5 9.3 %copy-start.40 = (s32[2]{0:T(128)S(1)}, s32[2]{0:T(128)}, u32[]{:S(2)}) copy-start(s32[2]{0:T(128)} %param.24) | copy-start | bytes 28
  124.8 49.6 %copy-start.9 = (f32[8,2]{1,0:T(8,128)}, f32[8,2]{1,0:T(8,128)S(1)}, u32[]{:S(2)}) copy-start(f32[8,2]{1,0:T(8,128)S(1)} %pad_maximum_fusion.2.far_ref.refs_1_) | copy-start | bytes 196
  124.9 49.5 %copy-start.10 = (s32[3]{0:T(128)}, s32[3]{0:T(128)S(1)}, u32[]{:S(2)}) copy-start(s32[3]{0:T(128)S(1)} %pad_add_fusion.1.info_ref.refs_0_) | copy-start | bytes 40
  144.1 1.0 copy-start.3
  145.1 0.8 copy-start.6
  145.9 28.4 %copy-start.2 = (f32[512,512]{1,0:T(8,128)}, f32[512,512]{1,0:T(8,128)S(1)}, u32[]{:S(2)}) copy-start(f32[512,512]{1,0:T(8,128)S(1)} %get-tuple-element.115.full_ref.refs_5_) | copy-start | bytes 3145732
  145.9 28.5 %copy-start.8 = (f32[2,4,2,256]{3,2,1,0:T(2,128)}, f32[2,4,2,256]{3,2,1,0:T(2,128)S(1)}, u32[]{:S(2)}) copy-start(f32[2,4,2,256]{3,2,1,0:T(2,128)S(1)} %get-tuple-element.116.peak_ref.refs_6_) | copy-start | bytes 49156
  145.9 26.8 %copy-start.34 = (s32[3,8,512]{2,1,0:T(8,128)S(1)}, s32[3,8,512]{2,1,0:T(8,128)}, u32[]{:S(2)}) copy-start(s32[3,8,512]{2,1,0:T(8,128)} %constant.264) | copy-start | bytes 147460
  170.1 25.6 %collective-permute-start = (bf16[4,2,16,4096]{3,2,1,0:T(8,128)(2,1)}, bf16[4,2,16,4096]{3,2,1,0:T(8,128)(2,1)}, u32[]{:S(2)}, u32[]{:S(2)}) collective-permute-start(bf16[4,2,16,4096]{3,2,1,0:T(8,128)(2,1)} %get-tuple-element.120), channel_id=1, source_target_pairs={{16,0},{24,8},{0,16},{8,24},{17,1},{25,9},{1,17},{9,25},{18,2},{26... | collective-permute-start | bytes 3145736 | tf_op jit(solution)/shard_map/ppermute | solution.py:1204
  174.4 1.0 copy-start.5
  194.9 0.7 copy-start
  271.5 2.3 copy-start.1
  271.5 2.3 copy-start.14
  271.5 2.3 copy-start.23
  271.5 2.3 copy-start.28
  273.8 2.0 copy-start.26
  276.1 1.5 copy-start.17
  277.6 5.3 %copy-start.12 = (f32[2,259,512]{2,1,0:T(8,128)S(1)}, f32[2,259,512]{2,1,0:T(8,128)}, u32[]{:S(2)}) copy-start(f32[2,259,512]{2,1,0:T(8,128)} %copy-done.11) | copy-start | bytes 3182596
  277.6 5.3 %copy-start.18 = (f32[2,256,512]{2,1,0:T(8,128)S(1)}, f32[2,256,512]{2,1,0:T(8,128)}, u32[]{:S(2)}) copy-start(f32[2,256,512]{2,1,0:T(8,128)} %get-tuple-element.168) | copy-start | bytes 3145732
  288.3 2.3 copy-start.19
  290.6 1.2 copy-start.20
  290.6 1.5 copy-start.21
  322.2 0.8 copy-start.38
  322.4 1.6 copy-start.33
  322.4 3.1 copy-start.27
  323.1 3.2 copy-start.32
  323.1 3.8 %copy-start.37 = (f32[16,512]{1,0:T(8,128)S(1)}, f32[16,512]{1,0:T(8,128)}, u32[]{:S(2)}) copy-start(f32[16,512]{1,0:T(8,128)} %get-tuple-element.217) | copy-start | bytes 98308
  323.1 4.4 %copy-start.36 = (f32[16,512]{1,0:T(8,128)S(1)}, f32[16,512]{1,0:T(8,128)}, u32[]{:S(2)}) copy-start(f32[16,512]{1,0:T(8,128)} %get-tuple-element.218) | copy-start | bytes 98308
  324.0 4.1 %copy-start.35 = (f32[16,512]{1,0:T(8,128)S(1)}, f32[16,512]{1,0:T(8,128)}, u32[]{:S(2)}) copy-start(f32[16,512]{1,0:T(8,128)} %get-tuple-element.221) | copy-start | bytes 98308
  324.0 4.8 %copy-start.31 = (f32[16,2048]{1,0:T(8,128)S(1)}, f32[16,2048]{1,0:T(8,128)}, u32[]{:S(2)}) copy-start(f32[16,2048]{1,0:T(8,128)} %get-tuple-element.223) | copy-start | bytes 393220
  324.0 5.4 %copy-start.30 = (f32[16,2048]{1,0:T(8,128)S(1)}, f32[16,2048]{1,0:T(8,128)}, u32[]{:S(2)}) copy-start(f32[16,2048]{1,0:T(8,128)} %get-tuple-element.224) | copy-start | bytes 393220
  324.0 6.1 %copy-start.29 = (f32[64,512]{1,0:T(8,128)S(1)}, f32[64,512]{1,0:T(8,128)}, u32[]{:S(2)}) copy-start(f32[64,512]{1,0:T(8,128)} %get-tuple-element.225) | copy-start | bytes 393220
where the time goes:
time: 336 us; the launch traced here: 331 us
  Pallas kernels  259 us (77%)
  local copies, waits for them, and re-layouts  28.8 us (9%)
  other arithmetic  24.6 us (7%)
  matrix products  15.1 us (4%)
    pallas_call x2, Pallas kernels, gather_all(): pl.pallas_call(functools.partial(gather_kernel, sizes, orders, int(rows i...  96.1 us
    pallas_call x1, Pallas kernels, back_rows(): pl.pallas_call(functools.partial(back_rows_kernel, sizes, rows, tasks_inf...  75.8 us
    pallas_call x1, Pallas kernels, reduce_all(): pl.pallas_call(functools.partial(reduce_kernel, sizes, orders, all_dims,...  24.4 us
    pallas_call x1, Pallas kernels, feed_forward(): pl.pallas_call(functools.partial(feed_forward_kernel, sizes), in_specs=[v...  24.2 us
    pallas_call x1, Pallas kernels, attend_back(): pl.pallas_call(functools.partial(attend_back_kernel, rows), grid=(pairs,...  19.5 us
    pallas_call x1, Pallas kernels, attend(): pl.pallas_call(functools.partial(attend_kernel, rows), grid=(pairs, seqs)...  19.2 us
    unnamed x95, local copies, waits for them, and re-layouts  13.3 us
    dot_general x3, matrix products, mat_dot(): return jnp.dot(lhs_array, rhs_array, preferred_element_type=jnp.float32)  10.1 us
  transfers between devices with their start and end apart: 1, of which 1 were waited for; matrix products, arithmetic and copies ran while one was open for 1% of the time, Pallas kernels for 6%

commit v1 on v0

--- a/solution.py
+++ b/solution.py
@@ -118,24 +118,16 @@
     return jnp.where(lane < half, block, zero), jnp.where(lane < half, zero, block)
 
 
-def attend_kernel(
-    rows, info_ref, far_ref, diag_ref, q_ref, k_ref, v_ref, o_ref, full_ref, inv_ref, peak_ref, bias_ref, s_ref, acc_ref
-):
-    pair, b = pl.program_id(0), pl.program_id(1)
-
-    @pl.when(b == 0)
-    def _():
-        fill_bias(rows, far_ref, diag_ref, bias_ref, pair)
-
-    length, first = info_ref[b], info_ref[pl.num_programs(1)]
-    count = lax.div(length + rows - 1, rows)
-    halves = head_halves(q_ref[...])
-    wide = q_ref.shape[1]
+def attend_pair(rows, length, first, q, keys, values, spans, bias_ref, s_ref, acc_ref):
+    halves = head_halves(q)
+    wide = q.shape[1]
     half = wide // 2
     key_row = lax.broadcasted_iota(jnp.int32, (rows, rows), 0)
-
-    def scores(kc, peaks):
-        k = k_ref[0, pl.ds(kc * rows, SPAN * rows), :]
+    lane = lax.broadcasted_iota(jnp.int32, (SPAN * rows, wide), 1)
+
+    def scores(i, peaks):
+        kc = i * SPAN
+        k = keys(pl.ds(kc * rows, SPAN * rows))
         new = list(peaks)
         for a in range(2):
             full = nt_dot(k, halves[a])
@@ -148,31 +140,53 @@
                 new[a] = jnp.maximum(new[a], jnp.max(s.reshape(rows // 8, 8, rows), axis=0))
         return tuple(new)
 
-    low = jnp.full((8, rows), -jnp.inf, jnp.float32)
-    spans = lax.div(count + SPAN - 1, SPAN)
-    peaks = lax.fori_loop(0, spans, lambda i, p: scores(i * SPAN, p), (low, low))
-    peaks = [jnp.max(p, axis=0, keepdims=True) for p in peaks]
-    acc_ref[...] = jnp.zeros_like(acc_ref)
-    lane = lax.broadcasted_iota(jnp.int32, (SPAN * rows, wide), 1)
-
     def weigh(i, carry):
         here = pl.ds(i * SPAN * rows, SPAN * rows)
-        v = v_ref[0, here, :]
+        v = values(here)
         ones = jnp.ones_like(v)
         for a, v_one in enumerate((jnp.where(lane < half, v, ones), jnp.where(lane < half, ones, v))):
-            e = jnp.exp(s_ref[a, here, :] - peaks[a])
+            e = jnp.exp(s_ref[a, here, :] - tops[a])
             acc_ref[a] += tn_dot(v_one, e.astype(jnp.bfloat16))
         return carry
 
-    lax.fori_loop(0, spans, weigh, 0)
+    low = jnp.full((8, rows), -jnp.inf, jnp.float32)
+    peaks = scores(0, (low, low)) if spans == 1 else lax.fori_loop(0, spans, scores, (low, low))
+    tops = [jnp.max(p, axis=0, keepdims=True) for p in peaks]
+    acc_ref[...] = jnp.zeros_like(acc_ref)
+    if spans == 1:
+        weigh(0, 0)
+    else:
+        lax.fori_loop(0, spans, weigh, 0)
     inv = jnp.concatenate([1.0 / acc_ref[0, half:], 1.0 / acc_ref[1, :half]], axis=0)
     out = jnp.concatenate([acc_ref[0, :half], acc_ref[1, half:]], axis=0) * inv
-    out = out.T
+    return out.T, inv.T, tops
+
+
+def attend_kernel(rows, skip, info_ref, far_ref, diag_ref, q_ref, k_ref, v_ref, *refs):
+    o_ref, full_ref, inv_ref, peak_ref, bias_ref, s_ref, acc_ref = refs
+    pair, b = pl.program_id(0), pl.program_id(1)
+
+    @pl.when(b == 0)
+    def _():
+        fill_bias(rows, far_ref, diag_ref, bias_ref, pair)
+
+    out, inv, tops = attend_pair(
+        rows,
+        info_ref[b + skip],
+        info_ref[info_ref.shape[0] - 1],
+        q_ref[...],
+        lambda here: k_ref[0, here, :],
+        lambda here: v_ref[0, here, :],
+        k_ref.shape[1] // (SPAN * rows),
+        bias_ref,
+        s_ref,
+        acc_ref,
+    )
     o_ref[...] = out.astype(o_ref.dtype)
     full_ref[...] = out
-    inv_ref[...] = inv.T
+    inv_ref[...] = inv
     for a in range(2):
-        peak_ref[0, 0, a : a + 1, :] = peaks[a]
+        peak_ref[0, 0, a : a + 1, :] = tops[a]
 
 
 def attention_cost(q, kv, products):
@@ -182,37 +196,43 @@
     )
 
 
-def attend(info, far, diag, q, kv, rows, length):
+def attention_shapes(seqs, rows, width, pairs):
+    shape = (seqs * rows, width)
+    return [
+        jax.ShapeDtypeStruct(shape, jnp.bfloat16),
+        jax.ShapeDtypeStruct(shape, jnp.float32),
+        jax.ShapeDtypeStruct(shape, jnp.float32),
+        jax.ShapeDtypeStruct((seqs, pairs, 2, rows), jnp.float32),
+    ]
+
+
+def attend(info, far, diag, q, kv, rows, length, skip):
     heads = far.shape[0]
     seqs = kv.shape[0]
     wide = 2 * (q.shape[1] // heads)
     pairs = heads // 2
     smem = pl.BlockSpec(memory_space=pltpu.SMEM)
     return pl.pallas_call(
-        functools.partial(attend_kernel, rows),
-        grid=(pairs, seqs),
+        functools.partial(attend_kernel, rows, skip),
+        grid=(pairs, seqs - skip),
         in_specs=[
-            smem, smem,
+            smem,
+            smem,
             pl.BlockSpec((1, 6, 2 * rows), lambda p, b: (p, 0, 0)),
-            pl.BlockSpec((rows, wide), lambda p, b: (b, p)),
-            pl.BlockSpec((1, length, wide), lambda p, b: (b, 0, 2 * p)),
-            pl.BlockSpec((1, length, wide), lambda p, b: (b, 0, 2 * p + 1)),
+            pl.BlockSpec((rows, wide), lambda p, b: (b + skip, p)),
+            pl.BlockSpec((1, length, wide), lambda p, b: (b + skip, 0, 2 * p)),
+            pl.BlockSpec((1, length, wide), lambda p, b: (b + skip, 0, 2 * p + 1)),
         ],
         out_specs=[pl.BlockSpec((rows, wide), lambda p, b: (b, p))] * 3
         + [pl.BlockSpec((1, 1, 2, rows), lambda p, b: (b, p, 0, 0))],
-        out_shape=[
-            jax.ShapeDtypeStruct(q.shape, jnp.bfloat16),
-            jax.ShapeDtypeStruct(q.shape, jnp.float32),
-            jax.ShapeDtypeStruct(q.shape, jnp.float32),
-            jax.ShapeDtypeStruct((seqs, pairs, 2, rows), jnp.float32),
-        ],
+        out_shape=attention_shapes(seqs - skip, rows, q.shape[1], pairs),
         scratch_shapes=[
             pltpu.VMEM((2, 5, rows, rows), jnp.float32),
             pltpu.VMEM((2, length, rows), jnp.float32),
             pltpu.VMEM((2, wide, rows), jnp.float32),
         ],
         compiler_params=pltpu.CompilerParams(vmem_limit_bytes=48 << 20),
-        cost_estimate=attention_cost(q, kv, 2),
+        cost_estimate=attention_cost(q, kv, 1),
         name="attend",
     )(info, far, diag, q, kv, kv)
 
@@ -505,58 +525,75 @@
             pl.when(cond)(send.wait_send)
 
 
-def spread_task(sizes, me, src, out, local_sem, sems):
+def spread_task(sizes, me, src, out, sems):
     z, y, n, fast = me["z"], me["y"], sizes["z"], sizes["y"]
-    own = pltpu.make_async_copy(src, out.at[:, z, y], local_sem)
-    own.start()
-    own.wait()
     fan = sems.take((fast - 1) * n)
-
-    def fan_copy(k, origin, owner):
-        peer = device_at(sizes, me, "y", lax.rem(y + k, fast))
-        spot = out.at[:, origin, owner]
-        return sems.copy(spot, spot, fan + (k - 1) * n + origin, peer)
+    base = sems.take(2 * (n - 1))
+
+    def fan_copy(k, origin, owner, to):
+        spot = out.at[origin, owner]
+        return sems.copy(spot, spot, fan + (k - 1) * n + origin, device_at(sizes, me, "y", to))
 
     def fan_out(origin):
         for k in range(1, fast):
-            fan_copy(k, origin, y).start()
-
-    fan_out(z)
-    sent = []
+            fan_copy(k, origin, y, lax.rem(y + k, fast)).start()
+
+    def along(origin, index, to):
+        spot = out.at[origin, y]
+        return sems.copy(spot, spot, base + index, device_at(sizes, me, "z", to))
+
+    moves = []
     for t in range(n - 1):
-        base = sems.take(2)
-        to_right = (z + 1 < n) & (z - t >= 0)
-        to_left = (z >= 1) & (z + t < n)
-        from_left = (z >= 1) & (z - 1 - t >= 0)
-        from_right = (z + 1 < n) & (z + 1 + t < n)
-        right = sems.copy(out.at[:, z - t, y], out.at[:, z - t, y], base, device_at(sizes, me, "z", z + 1))
-        left = sems.copy(out.at[:, z + t, y], out.at[:, z + t, y], base + 1, device_at(sizes, me, "z", z - 1))
-        pl.when(to_right)(right.start)
-        pl.when(to_left)(left.start)
-        sent += [(to_right, right), (to_left, left)]
+        moves.append(
+            (
+                (along(z - t, 2 * t, z + 1), (z + 1 < n) & (z - t >= 0)),
+                (along(z + t, 2 * t + 1, z - 1), (z >= 1) & (z + t < n)),
+                (along(z - 1 - t, 2 * t, z - 1), (z >= 1) & (z - 1 - t >= 0), z - 1 - t),
+                (along(z + 1 + t, 2 * t + 1, z + 1), (z + 1 < n) & (z + 1 + t < n), z + 1 + t),
+            )
+        )
+    fans = [fan_copy(k, origin, y, lax.rem(y + k, fast)) for k in range(1, fast) for origin in range(n)]
+
+    def begin(t):
+        for send, cond in moves[t][:2]:
+            pl.when(cond)(send.start)
+
+    def chains():
+        out[z, y] = src[...]
+        begin(0)
+        fan_out(z)
         yield
-
-        @pl.when(from_left)
-        def _():
-            spot = out.at[:, z - 1 - t, y]
-            sems.copy(spot, spot, base, device_at(sizes, me, "z", z - 1)).wait_recv()
-            fan_out(z - 1 - t)
-
-        @pl.when(from_right)
-        def _():
-            spot = out.at[:, z + 1 + t, y]
-            sems.copy(spot, spot, base + 1, device_at(sizes, me, "z", z + 1)).wait_recv()
-            fan_out(z + 1 + t)
-
-    yield
-    for k in range(1, fast):
-        for origin in range(n):
-            fan_copy(k, origin, lax.rem(y + fast - k, fast)).wait_recv()
-    for k in range(1, fast):
-        for origin in range(n):
-            fan_copy(k, origin, y).wait_send()
-    for cond, send in sent:
-        pl.when(cond)(send.wait_send)
+        for t in range(n - 1):
+            for got, cond, origin in moves[t][2:]:
+                pl.when(cond)(got.wait_recv)
+            if t + 1 < n - 1:
+                begin(t + 1)
+            for got, cond, origin in moves[t][2:]:
+                pl.when(cond)(partial(fan_out, origin))
+            yield
+        for send in fans:
+            send.wait_send()
+        for move in moves:
+            for send, cond in move[:2]:
+                pl.when(cond)(send.wait_send)
+
+    def across_y(use):
+        def step(i, carry):
+            far = lax.div(i + 1, 2)
+            origin = jnp.where(lax.rem(i, 2) == 1, z - far, z + far)
+
+            @pl.when((origin >= 0) & (origin < n))
+            def _():
+                for k in range(1, fast):
+                    owner = lax.rem(y + fast - k, fast)
+                    fan_copy(k, origin, owner, owner).wait_recv()
+                    use(origin, owner)
+
+            return carry
+
+        lax.fori_loop(0, 2 * n - 1, step, 0)
+
+    return chains(), across_y
 
 
 def shift_task(sizes, me, src, out, sems, step):
@@ -582,46 +619,43 @@
     return sum(1 if sizes[d] == 2 else 2 * (sizes[d] - 1) for d in order.lower())
 
 
-def gather_kernel(sizes, orders, has_rows, has_rim, plan, *refs):
+def gather_kernel(sizes, orders, has_rim, *refs):
     count = len(orders)
-    total = count + has_rows + has_rim
+    total = count + has_rim
     ins, outs = refs[:total], refs[total : 2 * total]
     local_sem, send_sem, recv_sem = refs[2 * total :]
     me = place(sizes)
-    used = [d for d in SLOTS if any(d in o.lower() for o in orders) or (has_rows and d in "zy")]
+    used = [d for d in SLOTS if any(d in o.lower() for o in orders)]
     greet(sizes, me, used + ["s"] * has_rim)
     sems = Sems(send_sem, recv_sem)
     tasks = []
     for i in range(count):
         tasks.append(gather_task(sizes, me, ins[i], outs[i], local_sem.at[i], sems, orders[i]))
-    if has_rows:
-        tasks.append(spread_task(sizes, me, ins[count], outs[count], local_sem.at[count], sems))
     if has_rim:
         tasks.append(shift_task(sizes, me, ins[-1], outs[-1], sems, 1))
-    run_together(tasks, plan)
-
-
-def gather_all(shards, orders, sizes, collective_id, rows=None, rim=None, plan=(), name="gather"):
-    ins, shapes, out_specs = [], [], []
+    run_together(tasks)
+
+
+def gather_shapes(shards, orders, sizes):
+    ins, shapes = [], []
     for shard, order in zip(shards, orders):
         ins.append(shard if shard.ndim > 2 else shard.reshape(tile_block(*shard.shape)))
         before = SLOTS[len(SLOTS) - (ins[-1].ndim - 2) :]
         whole = tuple(sizes[d] for d in SLOTS if d in order.lower() or d in before)
         shapes.append(jax.ShapeDtypeStruct(whole + ins[-1].shape[-2:], shard.dtype))
-    total = sum(stage_count(sizes, o) for o in orders)
+    return ins, shapes, sum(stage_count(sizes, o) for o in orders)
+
+
+def gather_all(shards, orders, sizes, collective_id, rim=None, name="gather"):
+    ins, shapes, total = gather_shapes(shards, orders, sizes)
     out_specs = [pl.BlockSpec(memory_space=pl.ANY)] * len(ins)
-    if rows is not None:
-        ins.append(rows)
-        shapes.append(jax.ShapeDtypeStruct((rows.shape[0], sizes["z"], sizes["y"]) + rows.shape[1:], rows.dtype))
-        out_specs.append(pl.BlockSpec(memory_space=pl.ANY))
-        total += (sizes["y"] - 1) * sizes["z"] + 2 * (sizes["z"] - 1)
     if rim is not None:
         ins.append(rim)
         shapes.append(jax.ShapeDtypeStruct(rim.shape, rim.dtype))
         out_specs.append(pl.BlockSpec(memory_space=pltpu.VMEM))
         total += 1
     return pl.pallas_call(
-        functools.partial(gather_kernel, sizes, orders, int(rows is not None), int(rim is not None), plan),
+        functools.partial(gather_kernel, sizes, orders, int(rim is not None)),
         in_specs=[pl.BlockSpec(memory_space=pltpu.VMEM)] * len(ins),
         out_specs=out_specs,
         out_shape=shapes,
@@ -633,6 +667,138 @@
         compiler_params=pltpu.CompilerParams(collective_id=collective_id, has_side_effects=True),
         name=name,
     )(*ins)
+
+
+def gather_rows_kernel(sizes, rows, orders, *refs):
+    count = len(orders)
+    info_ref, far_ref, diag_ref, rows_ref, q_ref, second_ref = refs[:6]
+    planes, refs = refs[6 : 6 + count], refs[6 + count :]
+    gathered, refs = refs[:count], refs[count:]
+    normed_out, kv_out, o_ref, full_ref, inv_ref, peak_ref = refs[:6]
+    rows_buf, kv_buf, bias_ref, s_ref, acc_ref, local_sem, out_sem, send_sem, recv_sem = refs[6:]
+    me = place(sizes)
+    greet(sizes, me, SLOTS)
+    sems = Sems(send_sem, recv_sem)
+    first = me["z"] * sizes["y"] + me["y"]
+    seqs, n = rows_ref.shape[0], sizes["z"]
+    length = kv_buf.shape[1]
+    pairs = diag_ref.shape[0]
+    wide = q_ref.shape[1] // pairs
+    weights = []
+    for i in range(count):
+        weights.append(gather_task(sizes, me, planes[i], gathered[i], local_sem.at[i], sems, orders[i]))
+        next(weights[-1])
+    pieces = [spread_task(sizes, me, rows_ref.at[p], rows_buf.at[p], sems) for p in range(seqs)]
+    begun, rest = pieces[0][0], [p[0] for p in pieces[1:]]
+    for _ in range(n):
+        next(begun)
+    for task in rest:
+        next(task)
+
+    def project(p):
+        def block(z, y):
+            at = pl.ds(pl.multiple_of((z * sizes["y"] + y) * rows, rows), rows)
+            kv_buf[p, at, :] = nn_dot(rows_buf[p, z, y], second_ref[...]).astype(jnp.bfloat16)
+
+        def column(z, carry):
+            block(z, me["y"])
+            return carry
+
+        lax.fori_loop(0, n, column, 0)
+        pieces[p][1](block)
+        copies = [
+            pltpu.make_async_copy(rows_buf.at[p], normed_out.at[p], out_sem.at[p, 0]),
+            pltpu.make_async_copy(kv_buf.at[p], kv_out.at[p], out_sem.at[p, 1]),
+        ]
+        for copy in copies:
+            copy.start()
+        return copies
+
+    copies = project(0)
+    size = info_ref[0]
+
+    def one_pair(p, carry):
+        fill_bias(rows, far_ref, diag_ref.at[pl.ds(p, 1)], bias_ref, p)
+        lanes = pl.ds(pl.multiple_of(p * wide, wide), wide)
+        k_lanes = pl.ds(pl.multiple_of(2 * p * wide, wide), wide)
+        v_lanes = pl.ds(pl.multiple_of((2 * p + 1) * wide, wide), wide)
+        out, inv, tops = attend_pair(
+            rows,
+            size,
+            first,
+            q_ref[:rows, lanes],
+            lambda here: kv_buf[0, here, k_lanes],
+            lambda here: kv_buf[0, here, v_lanes],
+            length // (SPAN * rows),
+            bias_ref,
+            s_ref,
+            acc_ref,
+        )
+        o_ref[:, lanes] = out.astype(o_ref.dtype)
+        full_ref[:, lanes] = out
+        inv_ref[:, lanes] = inv
+        for a in range(2):
+            peak_ref[0, p, a : a + 1, :] = tops[a]
+        for i in range(min(pairs, n - 1)):
+
+            @pl.when(p == i)
+            def _():
+                for task in rest:
+                    next(task)
+
+        return carry
+
+    lax.fori_loop(0, pairs, one_pair, 0)
+    for _ in range(n - 1 - min(pairs, n - 1)):
+        for task in rest:
+            next(task)
+    for task in weights:
+        next(task, None)
+    for p in range(1, seqs):
+        copies += project(p)
+    run_together(weights + [begun] + rest)
+    for copy in copies:
+        copy.wait()
+
+
+def gather_rows(info, far, diag, normed, queries, second, planes, orders, sizes, collective_id):
+    seqs, rows, width = normed.shape
+    n, fast = sizes["z"], sizes["y"]
+    length = rows * n * fast
+    pairs = far.shape[0] // 2
+    ins, shapes, total = gather_shapes(planes, orders, sizes)
+    total += seqs * ((fast - 1) * n + 2 * (n - 1))
+    bf16, f32 = jnp.bfloat16, jnp.float32
+    smem, vmem = pl.BlockSpec(memory_space=pltpu.SMEM), pl.BlockSpec(memory_space=pltpu.VMEM)
+    anywhere = pl.BlockSpec(memory_space=pl.ANY)
+    count = len(ins)
+    outs = pl.pallas_call(
+        functools.partial(gather_rows_kernel, sizes, rows, orders),
+        in_specs=[smem, smem] + [vmem] * (4 + count),
+        out_specs=[anywhere] * (count + 2) + [vmem] * 4,
+        out_shape=shapes
+        + [
+            jax.ShapeDtypeStruct((seqs, n, fast, rows, width), bf16),
+            jax.ShapeDtypeStruct((seqs, length, 2 * width), bf16),
+        ]
+        + attention_shapes(1, rows, width, pairs),
+        scratch_shapes=[
+            pltpu.VMEM((seqs, n, fast, rows, width), bf16),
+            pltpu.VMEM((seqs, length, 2 * width), bf16),
+            pltpu.VMEM((2, 5, rows, rows), f32),
+            pltpu.VMEM((2, length, rows), f32),
+            pltpu.VMEM((2, width // pairs, rows), f32),
+            pltpu.SemaphoreType.DMA((count,)),
+            pltpu.SemaphoreType.DMA((seqs, 2)),
+            pltpu.SemaphoreType.DMA((total,)),
+            pltpu.SemaphoreType.DMA((total,)),
+        ],
+        compiler_params=pltpu.CompilerParams(
+            collective_id=collective_id, has_side_effects=True, vmem_limit_bytes=60 << 20
+        ),
+        name="gather_rows",
+    )(info, far, diag, normed, queries, second, *ins)
+    return outs[:count], outs[count], outs[count + 1], outs[count + 2 :]
 
 
 def over(extents, body):
@@ -1073,10 +1239,14 @@
 
 def feed_forward_kernel(sizes, *refs):
     n = sizes["x"]
-    hidden_ref, att_ref, cot_ref, outer_ref, down_ref, gain_ref, inv_ref = refs[:7]
-    layer_ref, d_hidden_ref, d_out_ref, scaled_ref, d_gain_ref = refs[7:12]
-    wide_outs, down_out = refs[12 : 12 + n], refs[12 + n]
-    d_wide, d_down, wide_buf, down_buf, two_ref, low_ref, d_normed, send_sem, recv_sem = refs[13 + n :]
+    hidden_ref, cot_ref, outer_ref, down_ref, gain_ref = refs[:5]
+    att_parts, inv_parts, refs = refs[5:7], refs[7:9], refs[9:]
+    layer_ref, d_hidden_ref, d_out_ref, scaled_ref, d_gain_ref = refs[:5]
+    wide_outs, down_out = refs[5 : 5 + n], refs[5 + n]
+    d_wide, d_down, wide_buf, down_buf, two_ref, low_ref, d_normed, att_ref, send_sem, recv_sem = refs[6 + n :]
+    cut = att_parts[0].shape[0]
+    att_ref[:cut] = att_parts[0][...]
+    att_ref[cut:] = att_parts[1][...]
     me = place(sizes)
     greet(sizes, me, ("c",))
     sems = Sems(send_sem, recv_sem)
@@ -1142,7 +1312,8 @@
     d_low = d_two.astype(jnp.bfloat16)
     d_out_ref[...] = tn_dot(att_ref[...], d_low).astype(jnp.bfloat16)
     d_att = nt_dot(d_low, outer_ref[:, :width]).astype(jnp.bfloat16)
-    scaled_ref[...] = (d_att.astype(jnp.float32) * inv_ref[...]).astype(jnp.bfloat16)
+    scaled_ref[:cut] = (d_att[:cut].astype(jnp.float32) * inv_parts[0][...]).astype(jnp.bfloat16)
+    scaled_ref[cut:] = (d_att[cut:].astype(jnp.float32) * inv_parts[1][...]).astype(jnp.bfloat16)
     for send in sends:
         send.wait_recv()
     for x in range(n):
@@ -1153,7 +1324,7 @@
         send.wait_send()
 
 
-def feed_forward(hidden_one, attended, cotangent, outer_w, down_w, gain, inverse, sizes, collective_id):
+def feed_forward(hidden_one, cotangent, outer_w, down_w, gain, attended, inverse, sizes, collective_id):
     n = sizes["x"]
     whole = tuple(sizes[d] for d in SLOTS)
     devices = whole[0] * whole[1] * whole[2] * whole[3]
@@ -1166,7 +1337,7 @@
     vmem = pl.BlockSpec(memory_space=pltpu.VMEM)
     outs = pl.pallas_call(
         functools.partial(feed_forward_kernel, sizes),
-        in_specs=[vmem] * 7,
+        in_specs=[vmem] * 9,
         out_specs=[vmem] * (6 + n),
         out_shape=[
             jax.ShapeDtypeStruct((count, width), bf16),
@@ -1185,6 +1356,7 @@
             pltpu.VMEM((count, width), f32),
             pltpu.VMEM((count, width), bf16),
             pltpu.VMEM((count, width), f32),
+            pltpu.VMEM((count, width), bf16),
             pltpu.SemaphoreType.DMA((2 * n,)),
             pltpu.SemaphoreType.DMA((2 * n,)),
         ],
@@ -1192,7 +1364,7 @@
             collective_id=collective_id, has_side_effects=True, vmem_limit_bytes=60 << 20
         ),
         name="feed_forward",
-    )(hidden_one, attended, cotangent, outer_w, down_w, gain, inverse)
+    )(hidden_one, cotangent, outer_w, down_w, gain, *attended, *inverse)
     return list(outs[:5]) + [list(outs[5 : 5 + n]), outs[5 + n]]
 
 
@@ -1302,9 +1474,9 @@
             first,
             q_ref[tail, lanes],
             g_ref[tail, lanes],
-            full_ref[tail, lanes],
+            full_ref[:, lanes],
             (lambda here: (kv_buf[here, k_lanes], kv_buf[here, v_lanes]), length // (SPAN * rows)),
-            [peak_ref[last, p, a : a + 1, :] for a in range(2)],
+            [peak_ref[0, p, a : a + 1, :] for a in range(2)],
             bias_ref,
             sum_ref,
             acc_ref,
@@ -1556,34 +1728,45 @@
     normed_one, norm_one_back = jax.vjp(norm_rows, hidden_one, gain_first)
     normed_low = normed_one.astype(jnp.bfloat16)
 
-    outer_w, down_w, normed_all = gather_all(
+    queries = mat_dot(normed_low, query_w).astype(jnp.bfloat16)
+    far, diag = bias_tables(table, rows)
+    info = jnp.concatenate([lengths, lax.axis_index("seq")[None].astype(jnp.int32)])
+    (outer_w, down_w), normed_all, key_value, begun = gather_rows(
+        info,
+        far,
+        diag,
+        normed_low.reshape(seqs, rows, width),
+        queries,
+        second,
         [outer_plane, down_plane],
         ["xc", "xc"],
         sizes,
         2,
-        rows=normed_low.reshape(seqs, rows, width),
-        plan=(0, 1, 2, 2, 2, 2),
-        name="gather_rows",
     )
     outer_w = outer_w.reshape(width, -1)
     down_w = down_w.reshape(hidden, -1)
     out_w = outer_w[:, :width]
     wide_w = outer_w[:, width:]
     normed_all = normed_all.reshape(seqs * length, width)
-    queries = mat_dot(normed_low, query_w).astype(jnp.bfloat16)
-    key_value = mat_dot(normed_all, second).astype(jnp.bfloat16).reshape(seqs, length, 2 * width)
-
-    far, diag = bias_tables(table, rows)
-    info = jnp.concatenate([lengths, lax.axis_index("seq")[None].astype(jnp.int32)])
-    attended, attended_full, inverse, peak = attend(info, far, diag, queries, key_value, rows, length)
+    rest = attend(info, far, diag, queries, key_value, rows, length, 1)
 
     grad_low = cotangent.reshape(count, width)
     if own % 16 == 0:
         layer_out, d_hidden_two, d_out_w, scaled, d_gain_two, wide_pieces, down_half = feed_forward(
-            hidden_one, attended, grad_low, outer_w, down_w, gain_second[None], inverse, sizes, 4
+            hidden_one,
+            grad_low,
+            outer_w,
+            down_w,
+            gain_second[None],
+            (begun[0], rest[0]),
+            (begun[2], rest[2]),
+            sizes,
+            4,
         )
         d_gain_two = d_gain_two[0]
     else:
+        attended = jnp.concatenate([begun[0], rest[0]], axis=0)
+        inverse = jnp.concatenate([begun[2], rest[2]], axis=0)
         hidden_two = hidden_one + mat_dot(attended, out_w)
         normed_two, norm_two_back = jax.vjp(norm_rows, hidden_two, gain_second)
         normed_two_low = normed_two.astype(jnp.bfloat16)
@@ -1608,8 +1791,9 @@
     )
     wide_others = from_others(wide_pieces, sizes)
     early = seqs - 1
+    assert early == 1
     dq_before, dkv_before, near_before = attend_back(
-        info, far, diag, queries, scaled, attended_full, key_value, peak, rows, length, early
+        info, far, diag, queries, scaled, begun[1], key_value, begun[3], rows, length, early
     )
     dq_before, dkv_before, near_before, wide_others = lax.optimization_barrier(
         (dq_before, dkv_before, near_before, wide_others)
@@ -1620,9 +1804,9 @@
         diag,
         queries,
         scaled,
-        attended_full,
+        rest[1],
         key_value,
-        peak,
+        rest[3],
         dkv_before,
         normed_all,
         normed_low,

time: 336 us -> 325 us (0.967)
  matrix products: 15.1 us -> 5.36 us
  Pallas kernels: 259 us -> 255 us
    dot_general x3 -> x2, matrix products: 10.1 us -> 1.76 us  [mat_dot(): return jnp.dot(lhs_array, rhs_array, preferred_element_type=jnp.float32)]
    unnamed x95 -> x97, local copies, waits for them, and re-layouts: 13.3 us -> 14.1 us
where the time goes in v1:
time: 325 us; the launch traced here: 320 us
  Pallas kernels  255 us (78%)
  local copies, waits for them, and re-layouts  30.2 us (9%)
  other arithmetic  25.8 us (8%)
  matrix products  5.36 us (2%)
    pallas_call x1, Pallas kernels, back_rows(): pl.pallas_call(functools.partial(back_rows_kernel, sizes, rows, tasks_inf...  75.2 us
    pallas_call x1, Pallas kernels, gather_rows(): pl.pallas_call(functools.partial(gather_rows_kernel, sizes, rows, orders)...  59.3 us
    pallas_call x1, Pallas kernels, gather_all(): pl.pallas_call(functools.partial(gather_kernel, sizes, orders, int(rim is...  42.1 us
    pallas_call x1, Pallas kernels, reduce_all(): pl.pallas_call(functools.partial(reduce_kernel, sizes, orders, all_dims,...  24.4 us
    pallas_call x1, Pallas kernels, feed_forward(): pl.pallas_call(functools.partial(feed_forward_kernel, sizes), in_specs=[v...  23.7 us
    pallas_call x1, Pallas kernels, attend_back(): pl.pallas_call(functools.partial(attend_back_kernel, rows), grid=(pairs,...  19.5 us
    unnamed x97, local copies, waits for them, and re-layouts  14.1 us
    pallas_call x1, Pallas kernels, attend(): pl.pallas_call(functools.partial(attend_kernel, rows, skip), grid=(pairs,...  10.8 us
  transfers between devices with their start and end apart: 1, of which 1 were waited for; matrix products, arithmetic and copies ran while one was open for 1% of the time, Pallas kernels for 6%

profile of v1, /device:TPU:0, one launch (start us, length us, event | category | flops | bytes accessed | tf_op | source)
XLA Modules:
  0.0 320.0 jit_solution(17667165628201498533)
XLA Ops:
  0.7 0.8 stack_reshape.8
  1.4 0.7 stack_reshape.9
  2.3 0.6 reshape.268.refs_1_
  2.9 0.7 pad_bitcast_fusion
  3.7 0.7 copy.65
  4.4 0.7 copy.66
  5.1 1.4 slice.171.refs_4_
  6.5 1.5 pad_maximum_fusion.refs_2_
  8.1 1.5 concatenate.28.refs_0_
  9.5 42.1 %gather_first.1 = (bf16[2,2,4,2,16,1152]{5,4,3,2,1,0:T(8,128)(2,1)}, bf16[2,2,4,2,16,1024]{5,4,3,2,1,0:T(8,128)(2,1)}, bf16[4,2,16,4608]{3,2,1,0:T(8,128)(2,1)},...) custom-call(bf16[16,1152]{1,0:T(8,128)(2,1)} %concatenate.28.refs_0_, bf16[16,1024]{1,0:T(8,128)(2,1)} %reshape.268.refs_1_, ...), custom_call_target="tpu_custom_call" | custom-call | tf_op jit(solution)/shard_map/gather_first/pallas_call | solution.py:657
  51.6 0.9 slice.210
  52.5 1.4 fusion.39
  54.1 0.7 slice.174
  55.0 3.1 add_convert_fusion
  58.1 0.5 multiply_reduce_fusion.11
  59.2 1.2 convolution_convert_fusion.1.refs_4_.q_ref.refs_3_
  60.8 0.6 reshape.273.refs_2_.diag_ref
  61.5 0.7 pad_maximum_fusion.2.refs_1_.far_ref
  62.2 0.6 pad_add_fusion.1.refs_0_.info_ref
  62.8 59.3 %gather_rows.1 = (bf16[2,2,4,2,16,4608]{5,4,3,2,1,0:T(8,128)(2,1)}, bf16[2,2,4,2,64,512]{5,4,3,2,1,0:T(8,128)(2,1)}, bf16[2,4,2,256,512]{4,3,2,1,0:T(8,128)(2,1)...) custom-call(s32[3]{0:T(128)} %pad_add_fusion.1.refs_0_.info_ref, ...), custom_call_target="tpu_custom_call" | custom-call | tf_op jit(solution)/shard_map/gather_rows/pallas_call | solution.py:775
  122.1 10.8 %attend.1 = (bf16[256,512]{1,0:T(8,128)(2,1)S(1)}, f32[256,512]{1,0:T(8,128)S(1)}, f32[256,512]{1,0:T(8,128)S(1)}, f32[1,4,2,256]{3,2,1,0:T(2,128)S(1)}) custom-call(s32[3]{0:T(128)S(1)} %copy-done.10, f32[8,2]{1,0:T(8,128)S(1)} %copy-done.8, f32[4,6,512]{2,1,0:T(8,128)S(1)} %copy-done.1, bf16[512,512]{1,0:T(8,128)(2,1)S(1)} %copy-done, ...), custom_call_target="tpu_custom_call" | custom-call | flops 4294967296 | bytes 8912896 | tf_op jit(solution)/shard_map/attend/pallas_call | solution.py:215
  133.0 0.8 copy-done.4
  133.8 0.8 copy-done.6
  134.6 0.7 copy-done.7
  135.3 0.6 copy-done.9
  136.0 0.6 bitcast_convert_fusion.refs_4_
  136.6 23.7 %feed_forward.1 = (bf16[512,512]{1,0:T(8,128)(2,1)}, f32[512,512]{1,0:T(8,128)}, bf16[512,512]{1,0:T(8,128)(2,1)}, bf16[512,512]{1,0:T(8,128)(2,1)}, f32[1,512]{...) custom-call(f32[512,512]{1,0:T(8,128)} %copy-done.15, ...), custom_call_target="tpu_custom_call" | custom-call | tf_op jit(solution)/shard_map/feed_forward/pallas_call | solution.py:1338
  160.3 2.0 collective-permute-start
  162.3 0.6 compare_reduce_fusion
  163.0 0.9 iota_compare_fusion
  163.9 0.7 convert.28
  164.6 1.0 copy-done.5
  165.7 19.5 %attend_back.1 = (bf16[256,512]{1,0:T(8,128)(2,1)S(1)}, bf16[1,2048,1024]{2,1,0:T(8,128)(2,1)}, f32[4,2,5,8,512]{4,3,2,1,0:T(8,128)S(1)}) custom-call(s32[3]{0:T(128)S(1)} %copy-done.10, f32[8,2]{1,0:T(8,128)S(1)} %copy-done.8, f32[4,6,512]{2,1,0:T(8,128)S(1)} %copy-done.1, bf16[512,512]{1,0:T(8,128)(2,1)S(1)} %copy-done, bf16[512,512]{1,0:T(8,128)(2,1)S(1)} %copy-done.5, ...), custom_call_target="tpu_custom_call" | custom-call | flops 12884901888 | bytes 26738688 | tf_op jit(solution)/shard_map/attend_back/pallas_call | solution.py:343
  185.1 0.7 copy-done.2
  186.0 75.2 %back_rows.1 = (f32[2,256,512]{2,1,0:T(8,128)}, bf16[256,512]{1,0:T(8,128)(2,1)}, f32[4,2,5,8,512]{4,3,2,1,0:T(8,128)}, f32[16,2048]{1,0:T(8,128)}, f32[16,2048]...) custom-call(s32[3]{0:T(128)} %pad_add_fusion.1.refs_0_.info_ref, ...), custom_call_target="tpu_custom_call" | custom-call | tf_op jit(solution)/shard_map/back_rows/pallas_call | solution.py:1634
  261.2 1.3 add.212
  262.6 0.8 slice.232
  263.5 0.7 multiply_reduce_fusion
  264.3 0.5 copy-done.26
  265.1 1.5 fusion.26
  266.5 1.3 convolution_convert_fusion
  268.0 2.6 select_reduce_fusion
  270.6 0.7 add_select_fusion
  271.8 5.3 %multiply_reduce_fusion.9 = (f32[512]{0:T(512)S(1)}, f32[512]{0:T(512)S(1)}, f32[512]{0:T(512)S(1)}, f32[512]{0:T(512)S(1)}, f32[512]{0:T(512)S(1)}, /*index=5*/...) fusion(f32[2,259,512]{2,1,0:T(8,128)S(1)} %copy-done.14, ...), kind=kLoop, calls=%fused_computation.45 | loop fusion | flops 20442624 | bytes 10508288 | tf_op jit(solution)/shard_map/transpose(jvp())/reduce_sum | solution.py:63
  277.2 1.2 fusion.20
  278.4 1.1 copy.76
  279.7 1.0 copy-done.22
  281.0 0.9 broadcast_multiply_fusion
  282.0 1.2 pad_add_fusion
  283.2 0.6 slice.235.refs_2_
  283.8 24.4 %reduce.31 = (f32[16,512]{1,0:T(8,128)}, f32[16,128]{1,0:T(8,128)}, f32[16,512]{1,0:T(8,128)}, f32[16,512]{1,0:T(8,128)}, f32[16,1024]{1,0:T(8,128)}, /*index=5*/f32[2,8,512]{2,1,0:T(8,128)}) custom-call(bf16[2,2,4,2,16,640]{5,4,3,2,1,0:T(8,128)(2,1)} %bitcast.78, bf16[4,2,16,2048]{3,2,1,0:T(8,128)(2,1)} %get-tuple-element.142.refs_1_, ...), custom_call_target="tpu_custom_call" | custom-call | tf_op jit(solution)/shard_map/reduce/pallas_call | solution.py:1088
  308.2 1.5 slice_reduce_fusion.5
  309.6 1.4 slice_reduce_fusion.7
  312.0 0.9 convert_element_type.129
  313.1 0.6 copy.87
  313.7 0.6 copy.88
  314.3 0.8 copy.100
  315.1 0.6 copy.101
  315.7 0.6 copy.102
  316.4 0.6 copy.103
  317.0 0.6 copy.104
  317.6 0.7 copy.105
  318.3 0.7 copy.106
  318.9 0.7 copy.107
  (113 shorter events, 4.7 us)
Async XLA Ops:
  0.6 54.2 %copy-start.25 = (bf16[2,256,512]{2,1,0:T(8,128)(2,1)S(1)}, bf16[2,256,512]{2,1,0:T(8,128)(2,1)}, u32[]{:S(2)}) copy-start(bf16[2,256,512]{2,1,0:T(8,128)(2,1)} %param.23) | copy-start | bytes 1572868
  55.0 3.1 copy-start.13
  55.0 3.1 copy-start.24
  58.1 0.8 copy-start.18
  58.9 1.6 copy-start.15
  59.2 3.6 %copy-start.17 = (bf16[512,512]{1,0:T(8,128)(2,1)}, bf16[512,512]{1,0:T(8,128)(2,1)S(1)}, u32[]{:S(2)}) copy-start(bf16[512,512]{1,0:T(8,128)(2,1)S(1)} %multiply_convert_fusion.refs_11_) | copy-start | bytes 1572868
  59.2 1.5 copy-start.40
  59.2 3.0 copy-start.41
  62.7 59.3 %copy-start = (bf16[512,512]{1,0:T(8,128)(2,1)S(1)}, bf16[512,512]{1,0:T(8,128)(2,1)}, u32[]{:S(2)}) copy-start(bf16[512,512]{1,0:T(8,128)(2,1)} %convolution_convert_fusion.1.refs_4_.q_ref.refs_3_) | copy-start | bytes 1572868
  62.8 59.4 %copy-start.1 = (f32[4,6,512]{2,1,0:T(8,128)S(1)}, f32[4,6,512]{2,1,0:T(8,128)}, u32[]{:S(2)}) copy-start(f32[4,6,512]{2,1,0:T(8,128)} %reshape.273.refs_2_.diag_ref) | copy-start | bytes 147460
  62.8 59.4 %copy-start.8 = (f32[8,2]{1,0:T(8,128)S(1)}, f32[8,2]{1,0:T(8,128)}, u32[]{:S(2)}) copy-start(f32[8,2]{1,0:T(8,128)} %pad_maximum_fusion.2.refs_1_.far_ref) | copy-start | bytes 196
  62.8 59.4 %copy-start.10 = (s32[3]{0:T(128)S(1)}, s32[3]{0:T(128)}, u32[]{:S(2)}) copy-start(s32[3]{0:T(128)} %pad_add_fusion.1.refs_0_.info_ref) | copy-start | bytes 40
  133.0 0.8 copy-start.4
  133.8 0.8 copy-start.6
  134.6 0.7 copy-start.7
  135.3 0.6 copy-start.9
  136.6 26.4 %copy-start.35 = (s32[3,8,512]{2,1,0:T(8,128)S(1)}, s32[3,8,512]{2,1,0:T(8,128)}, u32[]{:S(2)}) copy-start(s32[3,8,512]{2,1,0:T(8,128)} %constant.264) | copy-start | bytes 147460
  136.6 28.0 %copy-start.11 = (f32[256,512]{1,0:T(8,128)S(1)}, f32[256,512]{1,0:T(8,128)}, u32[]{:S(2)}) copy-start(f32[256,512]{1,0:T(8,128)} %get-tuple-element.124.full_ref) | copy-start | bytes 1572868
  136.6 28.0 %copy-start.12 = (f32[1,4,2,256]{3,2,1,0:T(2,128)S(1)}, f32[1,4,2,256]{3,2,1,0:T(2,128)}, u32[]{:S(2)}) copy-start(f32[1,4,2,256]{3,2,1,0:T(2,128)} %get-tuple-element.125.peak_ref) | copy-start | bytes 24580
  160.3 25.7 %collective-permute-start = (bf16[4,2,16,4096]{3,2,1,0:T(8,128)(2,1)}, bf16[4,2,16,4096]{3,2,1,0:T(8,128)(2,1)}, u32[]{:S(2)}, u32[]{:S(2)}) collective-permute-start(bf16[4,2,16,4096]{3,2,1,0:T(8,128)(2,1)} %get-tuple-element.129), channel_id=1, source_target_pairs={{16,0},{24,8},{0,16},{8,24},{17,1},{25,9},{1,17},{9,25},{18,2},{26... | collective-permute-start | bytes 3145736 | tf_op jit(solution)/shard_map/ppermute | solution.py:1376
  164.6 1.0 copy-start.5
  185.1 0.7 copy-start.2
  261.2 2.3 copy-start.3
  261.2 2.3 copy-start.16
  261.2 2.3 copy-start.27
  261.2 2.3 copy-start.29
  263.5 1.2 copy-start.26
  265.1 1.5 copy-start.19
  266.5 5.3 %copy-start.14 = (f32[2,259,512]{2,1,0:T(8,128)S(1)}, f32[2,259,512]{2,1,0:T(8,128)}, u32[]{:S(2)}) copy-start(f32[2,259,512]{2,1,0:T(8,128)} %copy-done.13) | copy-start | bytes 3182596
  266.5 5.3 %copy-start.20 = (f32[2,256,512]{2,1,0:T(8,128)S(1)}, f32[2,256,512]{2,1,0:T(8,128)}, u32[]{:S(2)}) copy-start(f32[2,256,512]{2,1,0:T(8,128)} %get-tuple-element.178) | copy-start | bytes 3145732
  277.2 2.3 copy-start.21
  279.5 1.2 copy-start.22
  279.5 1.5 copy-start.23
  311.0 0.8 copy-start.39
  311.2 1.6 copy-start.34
  311.3 3.1 copy-start.28
  311.9 3.2 %copy-start.33 = (f32[16,128]{1,0:T(8,128)S(1)}, f32[16,128]{1,0:T(8,128)}, u32[]{:S(2)}) copy-start(f32[16,128]{1,0:T(8,128)} %get-tuple-element.144) | copy-start | bytes 24580
  311.9 3.8 %copy-start.38 = (f32[16,512]{1,0:T(8,128)S(1)}, f32[16,512]{1,0:T(8,128)}, u32[]{:S(2)}) copy-start(f32[16,512]{1,0:T(8,128)} %get-tuple-element.227) | copy-start | bytes 98308
  312.0 4.4 %copy-start.37 = (f32[16,512]{1,0:T(8,128)S(1)}, f32[16,512]{1,0:T(8,128)}, u32[]{:S(2)}) copy-start(f32[16,512]{1,0:T(8,128)} %get-tuple-element.228) | copy-start | bytes 98308
  312.8 4.1 %copy-start.36 = (f32[16,512]{1,0:T(8,128)S(1)}, f32[16,512]{1,0:T(8,128)}, u32[]{:S(2)}) copy-start(f32[16,512]{1,0:T(8,128)} %get-tuple-element.231) | copy-start | bytes 98308
  312.8 4.8 %copy-start.32 = (f32[16,2048]{1,0:T(8,128)S(1)}, f32[16,2048]{1,0:T(8,128)}, u32[]{:S(2)}) copy-start(f32[16,2048]{1,0:T(8,128)} %get-tuple-element.233) | copy-start | bytes 393220
  312.8 5.4 %copy-start.31 = (f32[16,2048]{1,0:T(8,128)S(1)}, f32[16,2048]{1,0:T(8,128)}, u32[]{:S(2)}) copy-start(f32[16,2048]{1,0:T(8,128)} %get-tuple-element.234) | copy-start | bytes 393220
  312.8 6.1 %copy-start.30 = (f32[64,512]{1,0:T(8,128)S(1)}, f32[64,512]{1,0:T(8,128)}, u32[]{:S(2)}) copy-start(f32[64,512]{1,0:T(8,128)} %get-tuple-element.235) | copy-start | bytes 393220

commit v2 on v1

--- a/solution.py
+++ b/solution.py
@@ -464,11 +464,23 @@
 
 
 def gather_task(sizes, me, src, out, local_sem, sems, order):
-    before = list(SLOTS[len(SLOTS) - (len(src.shape) - 2) :])
+    before = [] if isinstance(src, list) else list(SLOTS[len(SLOTS) - (len(src.shape) - 2) :])
     dims = [d for d in SLOTS if d in order.lower() or d in before]
-    own = pltpu.make_async_copy(src, out.at[tuple(me[d] for d in dims if d not in before)], local_sem)
-    own.start()
-    own.wait()
+    mine = out.at[tuple(me[d] for d in dims if d not in before)]
+    if isinstance(src, list):
+        first = 0
+        owns = []
+        for i, (ref, lo, hi) in enumerate(src):
+            owns.append(
+                pltpu.make_async_copy(ref.at[:, lo:hi], mine.at[:, first : first + hi - lo], local_sem.at[i])
+            )
+            first += hi - lo
+    else:
+        owns = [pltpu.make_async_copy(src, mine, local_sem.at[0])]
+    for own in owns:
+        own.start()
+    for own in owns:
+        own.wait()
     done = before
     sent = []
     for dim in order:
@@ -619,48 +631,63 @@
     return sum(1 if sizes[d] == 2 else 2 * (sizes[d] - 1) for d in order.lower())
 
 
-def gather_kernel(sizes, orders, has_rim, *refs):
+def gather_kernel(sizes, orders, cuts, has_rim, *refs):
     count = len(orders)
-    total = count + has_rim
-    ins, outs = refs[:total], refs[total : 2 * total]
-    local_sem, send_sem, recv_sem = refs[2 * total :]
+    arrays = sum(1 if cut is None else len(cut) for cut in cuts)
+    ins, outs = list(refs[: arrays + has_rim]), refs[arrays + has_rim : arrays + has_rim + count + has_rim]
+    local_sem, send_sem, recv_sem = refs[arrays + count + 2 * has_rim :]
     me = place(sizes)
     used = [d for d in SLOTS if any(d in o.lower() for o in orders)]
     greet(sizes, me, used + ["s"] * has_rim)
     sems = Sems(send_sem, recv_sem)
     tasks = []
     for i in range(count):
-        tasks.append(gather_task(sizes, me, ins[i], outs[i], local_sem.at[i], sems, orders[i]))
+        src = ins.pop(0) if cuts[i] is None else [(ins.pop(0), lo, hi) for lo, hi in cuts[i]]
+        tasks.append(gather_task(sizes, me, src, outs[i], local_sem.at[i], sems, orders[i]))
     if has_rim:
-        tasks.append(shift_task(sizes, me, ins[-1], outs[-1], sems, 1))
+        edge = ins[0].at[:, ins[0].shape[1] - outs[-1].shape[1] :, :]
+        tasks.append(shift_task(sizes, me, edge, outs[-1], sems, 1))
     run_together(tasks)
 
 
 def gather_shapes(shards, orders, sizes):
     ins, shapes = [], []
+    cuts = []
     for shard, order in zip(shards, orders):
+        if isinstance(shard, list) and shard[0][0].shape[0] % 16 == 0:
+            whole = tuple(sizes[d] for d in SLOTS if d in order.lower())
+            block = (shard[0][0].shape[0], sum(hi - lo for _, lo, hi in shard))
+            shapes.append(jax.ShapeDtypeStruct(whole + block, shard[0][0].dtype))
+            ins += [piece for piece, _, _ in shard]
+            cuts.append([(lo, hi) for _, lo, hi in shard])
+            continue
+        if isinstance(shard, list):
+            shard = jnp.concatenate([piece[:, lo:hi] for piece, lo, hi in shard], axis=1)
         ins.append(shard if shard.ndim > 2 else shard.reshape(tile_block(*shard.shape)))
         before = SLOTS[len(SLOTS) - (ins[-1].ndim - 2) :]
         whole = tuple(sizes[d] for d in SLOTS if d in order.lower() or d in before)
         shapes.append(jax.ShapeDtypeStruct(whole + ins[-1].shape[-2:], shard.dtype))
-    return ins, shapes, sum(stage_count(sizes, o) for o in orders)
+        cuts.append(None)
+    return ins, shapes, sum(stage_count(sizes, o) for o in orders), cuts
 
 
 def gather_all(shards, orders, sizes, collective_id, rim=None, name="gather"):
-    ins, shapes, total = gather_shapes(shards, orders, sizes)
-    out_specs = [pl.BlockSpec(memory_space=pl.ANY)] * len(ins)
+    ins, shapes, total, cuts = gather_shapes(shards, orders, sizes)
+    out_specs = [pl.BlockSpec(memory_space=pl.ANY)] * len(shapes)
+    in_specs = [pl.BlockSpec(memory_space=pltpu.VMEM)] * len(ins)
     if rim is not None:
         ins.append(rim)
-        shapes.append(jax.ShapeDtypeStruct(rim.shape, rim.dtype))
+        in_specs.append(pl.BlockSpec(memory_space=pl.ANY))
+        shapes.append(jax.ShapeDtypeStruct((rim.shape[0], 16, rim.shape[2]), rim.dtype))
         out_specs.append(pl.BlockSpec(memory_space=pltpu.VMEM))
         total += 1
     return pl.pallas_call(
-        functools.partial(gather_kernel, sizes, orders, int(rim is not None)),
-        in_specs=[pl.BlockSpec(memory_space=pltpu.VMEM)] * len(ins),
+        functools.partial(gather_kernel, sizes, orders, cuts, int(rim is not None)),
+        in_specs=in_specs,
         out_specs=out_specs,
         out_shape=shapes,
         scratch_shapes=[
-            pltpu.SemaphoreType.DMA((len(ins),)),
+            pltpu.SemaphoreType.DMA((len(orders), len(ins))),
             pltpu.SemaphoreType.DMA((total,)),
             pltpu.SemaphoreType.DMA((total,)),
         ],
@@ -766,7 +793,7 @@
     n, fast = sizes["z"], sizes["y"]
     length = rows * n * fast
     pairs = far.shape[0] // 2
-    ins, shapes, total = gather_shapes(planes, orders, sizes)
+    ins, shapes, total, _ = gather_shapes(planes, orders, sizes)
     total += seqs * ((fast - 1) * n + 2 * (n - 1))
     bf16, f32 = jnp.bfloat16, jnp.float32
     smem, vmem = pl.BlockSpec(memory_space=pltpu.SMEM), pl.BlockSpec(memory_space=pltpu.VMEM)
@@ -788,7 +815,7 @@
             pltpu.VMEM((2, 5, rows, rows), f32),
             pltpu.VMEM((2, length, rows), f32),
             pltpu.VMEM((2, width // pairs, rows), f32),
-            pltpu.SemaphoreType.DMA((count,)),
+            pltpu.SemaphoreType.DMA((count, 1)),
             pltpu.SemaphoreType.DMA((seqs, 2)),
             pltpu.SemaphoreType.DMA((total,)),
             pltpu.SemaphoreType.DMA((total,)),
@@ -1658,6 +1685,53 @@
     return heads + results + [outs[0], inner is not None]
 
 
+def finish_kernel(refs_in, *refs):
+    layer, d_inputs, spill, small, proj, query, out, second, gate, up, down = refs[:refs_in]
+    (o_layer, o_input, o_taps, o_proj, o_query, o_key, o_value, o_out, o_gate, o_up, o_down) = refs[refs_in:]
+    o_layer[...] = layer[...]
+    rows = d_inputs.shape[1]
+    edge = lax.broadcasted_iota(jnp.int32, spill.shape[1:], 0)
+    for b in range(d_inputs.shape[0]):
+        o_input[b] = d_inputs[b].astype(o_input.dtype)
+        late = jnp.where(edge >= 5, pltpu.roll(spill[b], 5, 0), 0.0)
+        tail = d_inputs[b, rows - 16 :, :]
+        late = jnp.concatenate([jnp.zeros_like(late), late], axis=0)
+        o_input[b, rows - 16 :, :] = (tail + late).astype(o_input.dtype)
+    o_taps[...] = small[:, :TAPS]
+    for source, target in ((proj, o_proj), (query, o_query), (out, o_out), (gate, o_gate), (up, o_up), (down, o_down)):
+        target[...] = source[...]
+    pair = PACK
+    for p in range(second.shape[1] // (2 * pair)):
+        o_key[:, p * pair : (p + 1) * pair] = second[:, 2 * p * pair : (2 * p + 1) * pair]
+        o_value[:, p * pair : (p + 1) * pair] = second[:, (2 * p + 1) * pair : (2 * p + 2) * pair]
+
+
+def finish(*ins):
+    layer, d_inputs, _, small, proj, query, out, second, gate, up, down = ins
+    like = lambda x: jax.ShapeDtypeStruct(x.shape, x.dtype)
+    vmem = pl.BlockSpec(memory_space=pltpu.VMEM)
+    return pl.pallas_call(
+        functools.partial(finish_kernel, len(ins)),
+        in_specs=[vmem] * len(ins),
+        out_specs=[vmem] * 11,
+        out_shape=[
+            like(layer),
+            jax.ShapeDtypeStruct(d_inputs.shape, jnp.bfloat16),
+            jax.ShapeDtypeStruct((small.shape[0], TAPS), jnp.float32),
+            like(proj),
+            like(query),
+            like(proj),
+            like(proj),
+            like(out),
+            like(gate),
+            like(up),
+            like(down),
+        ],
+        compiler_params=pltpu.CompilerParams(vmem_limit_bytes=32 << 20),
+        name="finish",
+    )(*ins)
+
+
 def on_device(
     inputs,
     lengths,
@@ -1697,18 +1771,21 @@
         axis=1,
     )
     pairs = heads // 2
-    key_value_w = jnp.stack([w_key.reshape(own, pairs, -1), w_value.reshape(own, pairs, -1)], axis=2)
+    pair = width // pairs
+    key_value_w = []
+    for p in range(pairs):
+        key_value_w += [(w_key, p * pair, (p + 1) * pair), (w_value, p * pair, (p + 1) * pair)]
     first, second, outer_plane, down_plane, left_rim = gather_all(
         [
-            jnp.concatenate([small, w_proj, w_query], axis=1),
-            key_value_w.reshape(own, -1),
-            jnp.concatenate([w_out, w_gate, w_up], axis=1),
+            [(small, 0, PACK), (w_proj, 0, width), (w_query, 0, width)],
+            key_value_w,
+            [(w_out, 0, width), (w_gate, 0, hidden), (w_up, 0, hidden)],
             w_down,
         ],
         ["Zyxc", "Zxyc", "zy", "yz"],
         sizes,
         1,
-        rim=inputs[:, rows - 16 :, :],
+        rim=inputs,
         name="gather_first",
     )
     first = first.reshape(width, -1)
@@ -1857,22 +1934,35 @@
         spill=d_padded[:, :8, :],
         splits=[(width, PACK), (width, width, 2 * width)],
     )
-    input_grad = d_inputs.at[:, rows - 3 :, :].add(spill[:, :3]).astype(jnp.bfloat16)
-    g_second = g_second.reshape(own, pairs, 2, -1)
+    assert pair == PACK
+    done = finish(
+        layer_out,
+        d_inputs,
+        spill,
+        g_small,
+        g_proj,
+        g_query,
+        g_out,
+        g_second,
+        g_gate,
+        g_up,
+        g_down.reshape(w_down.shape),
+    )
+    layer_out, input_grad, g_taps, g_proj, g_query, g_key, g_value, g_out, g_gate, g_up, g_down = done
     return (
         layer_out.reshape(seqs, rows, width),
         input_grad,
-        g_small[:, :TAPS],
+        g_taps,
         g_small[:, TAPS],
         g_proj,
         g_query,
-        g_second[:, :, 0].reshape(own, width),
-        g_second[:, :, 1].reshape(own, width),
+        g_key,
+        g_value,
         g_out,
         g_small[:, TAPS + 1],
         g_gate,
         g_up,
-        g_down.reshape(w_down.shape),
+        g_down,
         g_small[:own_bias, TAPS + 2],
     )
 

time: 325 us -> 315 us (0.969)
  local copies, waits for them, and re-layouts: 30.2 us -> 21.3 us
    unnamed x97 -> x87, local copies, waits for them, and re-layouts: 14.1 us -> 9.2 us
    pallas_call x1 -> x2, Pallas kernels: 42.1 us -> 44 us  [the longest x1 42.7 us: gather_all(): pl.pallas_call(functools.partial(gather_kernel, sizes, orders, cuts, int(...]
where the time goes in v2:
time: 315 us; the launch traced here: 311 us
  Pallas kernels  257 us (82%)
  other arithmetic  23.9 us (8%)
  local copies, waits for them, and re-layouts  21.3 us (7%)
  matrix products  5.33 us (2%)
    pallas_call x1, Pallas kernels, back_rows(): pl.pallas_call(functools.partial(back_rows_kernel, sizes, rows, tasks_inf...  74.5 us
    pallas_call x1, Pallas kernels, gather_rows(): pl.pallas_call(functools.partial(gather_rows_kernel, sizes, rows, orders)...  59.6 us
    pallas_call x1, Pallas kernels, gather_all(): pl.pallas_call(functools.partial(gather_kernel, sizes, orders, cuts, int(...  42.7 us
    pallas_call x1, Pallas kernels, reduce_all(): pl.pallas_call(functools.partial(reduce_kernel, sizes, orders, all_dims,...  24.4 us
    pallas_call x1, Pallas kernels, feed_forward(): pl.pallas_call(functools.partial(feed_forward_kernel, sizes), in_specs=[v...  23.7 us
    pallas_call x1, Pallas kernels, attend_back(): pl.pallas_call(functools.partial(attend_back_kernel, rows), grid=(pairs,...  19.5 us
    pallas_call x1, Pallas kernels, attend(): pl.pallas_call(functools.partial(attend_kernel, rows, skip), grid=(pairs,...  10.8 us
    unnamed x87, local copies, waits for them, and re-layouts  9.2 us
  transfers between devices with their start and end apart: 1, of which 1 were waited for; matrix products, arithmetic and copies ran while one was open for 1% of the time, Pallas kernels for 6%

profile of v2, /device:TPU:0, one launch (start us, length us, event | category | flops | bytes accessed | tf_op | source)
XLA Modules:
  0.0 310.6 jit_solution(7006527717973938897)
XLA Ops:
  0.7 0.7 pad_bitcast_fusion
  1.4 0.1 copy.61
  1.5 0.7 copy.59
  2.2 0.7 copy.60
  3.0 1.4 concatenate.23.refs_0_
  4.3 42.7 %gather_first.1 = (bf16[2,2,4,2,16,1152]{5,4,3,2,1,0:T(8,128)(2,1)}, bf16[2,2,4,2,16,1024]{5,4,3,2,1,0:T(8,128)(2,1)}, bf16[4,2,16,4608]{3,2,1,0:T(8,128)(2,1)},...) custom-call(bf16[16,128]{1,0:T(8,128)(2,1)} %concatenate.23.refs_0_, bf16[16,512]{1,0:T(8,128)(2,1)} %refs_1_.1, ...), custom_call_target="tpu_custom_call" | custom-call | tf_op jit(solution)/shard_map/gather_first/pallas_call | solution.py:684
  47.1 0.9 slice.165
  48.0 2.1 fusion.39
  50.1 0.1 copy.69
  50.2 0.7 slice.134
  50.9 0.1 maximum_convert_fusion
  51.1 3.1 add_convert_fusion
  54.2 0.5 multiply_reduce_fusion.11
  54.7 0.3 copy-done.29
  55.0 1.2 copy.74
  56.2 0.2 multiply_convert_fusion.refs_11_
  56.4 1.2 convolution_convert_fusion.1.refs_4_.q_ref.refs_3_
  57.9 0.2 fusion.31
  58.1 0.6 reshape.237.refs_2_.diag_ref
  58.7 0.7 pad_maximum_fusion.refs_1_.far_ref
  59.4 0.6 pad_add_fusion.1.refs_0_.info_ref
  60.0 59.6 %gather_rows.1 = (bf16[2,2,4,2,16,4608]{5,4,3,2,1,0:T(8,128)(2,1)}, bf16[2,2,4,2,64,512]{5,4,3,2,1,0:T(8,128)(2,1)}, bf16[2,4,2,256,512]{4,3,2,1,0:T(8,128)(2,1)...) custom-call(s32[3]{0:T(128)} %pad_add_fusion.1.refs_0_.info_ref, ...), custom_call_target="tpu_custom_call" | custom-call | tf_op jit(solution)/shard_map/gather_rows/pallas_call | solution.py:802
  119.6 10.8 %attend.1 = (bf16[256,512]{1,0:T(8,128)(2,1)S(1)}, f32[256,512]{1,0:T(8,128)S(1)}, f32[256,512]{1,0:T(8,128)S(1)}, f32[1,4,2,256]{3,2,1,0:T(2,128)S(1)}) custom-call(s32[3]{0:T(128)S(1)} %copy-done.20, f32[8,2]{1,0:T(8,128)S(1)} %copy-done.14, f32[4,6,512]{2,1,0:T(8,128)S(1)} %copy-done.1, bf16[512,512]{1,0:T(8,128)(2,1)S(1)} %copy-done, ...), custom_call_target="tpu_custom_call" | custom-call | flops 4294967296 | bytes 8912896 | tf_op jit(solution)/shard_map/attend/pallas_call | solution.py:215
  130.5 0.8 copy-done.4
  131.3 0.8 copy-done.7
  132.1 0.7 copy-done.8
  132.8 0.6 copy-done.19
  133.4 0.1 copy.72
  133.5 0.6 bitcast_convert_fusion.refs_4_
  134.1 23.7 %feed_forward.1 = (bf16[512,512]{1,0:T(8,128)(2,1)}, f32[512,512]{1,0:T(8,128)}, bf16[512,512]{1,0:T(8,128)(2,1)}, bf16[512,512]{1,0:T(8,128)(2,1)}, f32[1,512]{...) custom-call(f32[512,512]{1,0:T(8,128)} %copy-done.25, ...), custom_call_target="tpu_custom_call" | custom-call | tf_op jit(solution)/shard_map/feed_forward/pallas_call | solution.py:1365
  157.9 1.3 collective-permute-start
  159.2 0.6 compare_reduce_fusion
  159.8 1.0 iota_compare_fusion
  160.8 0.7 convert.28
  161.5 1.0 copy-done.5
  162.5 19.5 %attend_back.1 = (bf16[256,512]{1,0:T(8,128)(2,1)S(1)}, bf16[1,2048,1024]{2,1,0:T(8,128)(2,1)}, f32[4,2,5,8,512]{4,3,2,1,0:T(8,128)S(1)}) custom-call(s32[3]{0:T(128)S(1)} %copy-done.20, f32[8,2]{1,0:T(8,128)S(1)} %copy-done.14, f32[4,6,512]{2,1,0:T(8,128)S(1)} %copy-done.1, bf16[512,512]{1,0:T(8,128)(2,1)S(1)} %copy-done, bf16[512,512]{1,0:T(8,128)(2,1)S(1)} %copy-done.5, ...), custom_call_target="tpu_custom_call" | custom-call | flops 12884901888 | bytes 26738688 | tf_op jit(solution)/shard_map/attend_back/pallas_call | solution.py:343
  182.0 0.7 copy-done.2
  182.7 0.6 collective-permute-done.refs_15_
  183.3 74.5 %back_rows.1 = (f32[2,256,512]{2,1,0:T(8,128)}, bf16[256,512]{1,0:T(8,128)(2,1)}, f32[4,2,5,8,512]{4,3,2,1,0:T(8,128)}, f32[16,2048]{1,0:T(8,128)}, f32[16,2048]...) custom-call(s32[3]{0:T(128)} %pad_add_fusion.1.refs_0_.info_ref, ...), custom_call_target="tpu_custom_call" | custom-call | tf_op jit(solution)/shard_map/back_rows/pallas_call | solution.py:1661
  257.9 1.3 add.205
  259.2 0.8 slice.186
  260.0 0.1 slice_reduce_fusion
  260.2 0.7 multiply_reduce_fusion
  260.9 0.5 copy-done.36
  261.4 0.3 fusion.19
  261.7 1.4 fusion.26
  263.2 1.3 convolution_convert_fusion
  264.6 2.6 select_reduce_fusion
  267.2 0.7 add_select_fusion
  268.4 5.3 %multiply_reduce_fusion.9 = (f32[512]{0:T(512)S(1)}, f32[512]{0:T(512)S(1)}, f32[512]{0:T(512)S(1)}, f32[512]{0:T(512)S(1)}, f32[512]{0:T(512)S(1)}, /*index=5*/...) fusion(f32[2,259,512]{2,1,0:T(8,128)S(1)} %copy-done.24, ...), kind=kLoop, calls=%fused_computation.45 | loop fusion | flops 20442624 | bytes 10508288 | tf_op jit(solution)/shard_map/transpose(jvp())/reduce_sum | solution.py:63
  273.8 1.2 fusion.20
  275.0 1.1 copy.68
  276.1 0.3 broadcast_multiply_fusion.7
  276.4 1.0 copy-done.33
  277.3 0.3 copy-done.34
  277.6 0.9 broadcast_multiply_fusion
  278.6 1.2 pad_add_fusion
  279.8 0.6 slice.189.refs_2_
  280.4 24.4 %reduce.21 = (f32[16,512]{1,0:T(8,128)}, f32[16,128]{1,0:T(8,128)}, f32[16,512]{1,0:T(8,128)}, f32[16,512]{1,0:T(8,128)}, f32[16,1024]{1,0:T(8,128)}, /*index=5*/f32[2,8,512]{2,1,0:T(8,128)}) custom-call(bf16[2,2,4,2,16,640]{5,4,3,2,1,0:T(8,128)(2,1)} %bitcast.70, bf16[4,2,16,2048]{3,2,1,0:T(8,128)(2,1)} %get-tuple-element.141.refs_1_, ...), custom_call_target="tpu_custom_call" | custom-call | tf_op jit(solution)/shard_map/reduce/pallas_call | solution.py:1115
  304.8 1.5 slice_reduce_fusion.3
  306.3 1.4 slice_reduce_fusion.5
  307.8 0.2 slice_add_fusion.refs_1_
  308.0 0.7 copy-done.6
  308.9 1.3 finish.1
  (93 shorter events, 1.2 us)
Async XLA Ops:
  0.6 50.3 %copy-start.28 = (bf16[2,256,512]{2,1,0:T(8,128)(2,1)S(1)}, bf16[2,256,512]{2,1,0:T(8,128)(2,1)}, u32[]{:S(2)}) copy-start(bf16[2,256,512]{2,1,0:T(8,128)(2,1)} %refs_15_.1) | copy-start | bytes 1572868
  51.1 3.1 copy-start.23
  51.1 3.1 copy-start.35
  54.2 0.8 copy-start.29
  55.0 2.7 copy-start.25
  56.4 3.6 %copy-start.27 = (bf16[512,512]{1,0:T(8,128)(2,1)}, bf16[512,512]{1,0:T(8,128)(2,1)S(1)}, u32[]{:S(2)}) copy-start(bf16[512,512]{1,0:T(8,128)(2,1)S(1)} %multiply_convert_fusion.refs_11_) | copy-start | bytes 1572868
  56.4 1.5 copy-start.40
  56.4 3.0 copy-start.41
  60.0 59.6 %copy-start = (bf16[512,512]{1,0:T(8,128)(2,1)S(1)}, bf16[512,512]{1,0:T(8,128)(2,1)}, u32[]{:S(2)}) copy-start(bf16[512,512]{1,0:T(8,128)(2,1)} %convolution_convert_fusion.1.refs_4_.q_ref.refs_3_) | copy-start | bytes 1572868
  60.0 59.6 %copy-start.1 = (f32[4,6,512]{2,1,0:T(8,128)S(1)}, f32[4,6,512]{2,1,0:T(8,128)}, u32[]{:S(2)}) copy-start(f32[4,6,512]{2,1,0:T(8,128)} %reshape.237.refs_2_.diag_ref) | copy-start | bytes 147460
  60.0 59.6 %copy-start.14 = (f32[8,2]{1,0:T(8,128)S(1)}, f32[8,2]{1,0:T(8,128)}, u32[]{:S(2)}) copy-start(f32[8,2]{1,0:T(8,128)} %pad_maximum_fusion.refs_1_.far_ref) | copy-start | bytes 196
  60.0 59.6 %copy-start.20 = (s32[3]{0:T(128)S(1)}, s32[3]{0:T(128)}, u32[]{:S(2)}) copy-start(s32[3]{0:T(128)} %pad_add_fusion.1.refs_0_.info_ref) | copy-start | bytes 40
  130.4 0.8 copy-start.4
  131.3 0.8 copy-start.7
  132.1 0.7 copy-start.8
  132.8 0.6 copy-start.19
  134.1 25.7 %copy-start.39 = (s32[3,8,512]{2,1,0:T(8,128)S(1)}, s32[3,8,512]{2,1,0:T(8,128)}, u32[]{:S(2)}) copy-start(s32[3,8,512]{2,1,0:T(8,128)} %constant.236) | copy-start | bytes 147460
  134.1 27.3 %copy-start.21 = (f32[256,512]{1,0:T(8,128)S(1)}, f32[256,512]{1,0:T(8,128)}, u32[]{:S(2)}) copy-start(f32[256,512]{1,0:T(8,128)} %get-tuple-element.123.full_ref) | copy-start | bytes 1572868
  134.1 27.3 %copy-start.22 = (f32[1,4,2,256]{3,2,1,0:T(2,128)S(1)}, f32[1,4,2,256]{3,2,1,0:T(2,128)}, u32[]{:S(2)}) copy-start(f32[1,4,2,256]{3,2,1,0:T(2,128)} %get-tuple-element.124.peak_ref) | copy-start | bytes 24580
  157.9 25.5 %collective-permute-start = (bf16[4,2,16,4096]{3,2,1,0:T(8,128)(2,1)}, bf16[4,2,16,4096]{3,2,1,0:T(8,128)(2,1)}, u32[]{:S(2)}, u32[]{:S(2)}) collective-permute-start(bf16[4,2,16,4096]{3,2,1,0:T(8,128)(2,1)} %get-tuple-element.128), channel_id=1, source_target_pairs={{16,0},{24,8},{0,16},{8,24},{17,1},{25,9},{1,17},{9,25},{18,2},{26... | collective-permute-start | bytes 3145736 | tf_op jit(solution)/shard_map/ppermute | solution.py:1403
  161.5 1.0 copy-start.5
  182.0 0.7 copy-start.2
  257.8 2.3 copy-start.3
  257.8 2.3 copy-start.26
  257.8 2.3 copy-start.37
  257.8 2.3 copy-start.38
  260.2 1.2 copy-start.36
  261.7 1.5 copy-start.30
  263.2 5.3 %copy-start.24 = (f32[2,259,512]{2,1,0:T(8,128)S(1)}, f32[2,259,512]{2,1,0:T(8,128)}, u32[]{:S(2)}) copy-start(f32[2,259,512]{2,1,0:T(8,128)} %copy-done.23) | copy-start | bytes 3182596
  263.2 5.3 %copy-start.31 = (f32[2,256,512]{2,1,0:T(8,128)S(1)}, f32[2,256,512]{2,1,0:T(8,128)}, u32[]{:S(2)}) copy-start(f32[2,256,512]{2,1,0:T(8,128)} %get-tuple-element.186) | copy-start | bytes 3145732
  273.8 2.3 copy-start.32
  276.1 1.2 copy-start.33
  276.1 1.5 copy-start.34
  307.7 1.0 copy-start.6
  307.7 1.1 copy-start.9
  307.7 1.1 copy-start.10
  307.7 1.1 copy-start.11
  307.7 1.1 copy-start.12
  307.7 1.1 copy-start.13
  307.7 1.1 copy-start.15
  307.7 1.1 copy-start.16
  307.7 1.1 copy-start.17
  307.8 1.1 copy-start.18

commit v3 on v2

--- a/solution.py
+++ b/solution.py
@@ -1412,7 +1412,7 @@
         del refs[:count]
         return taken
 
-    info_ref, far_ref, diag_ref, q_ref, g_ref, full_ref, peak_ref, kv_ref, dkv_ref, normed_ref, second_ref = take(11)
+    info_ref, far_ref, diag_ref, q_ref, g_ref, full_ref, peak_ref, kv_ref, dkv_ref, normed_ref, second_ref, near_before = take(12)
     if inner:
         own_ref, dq_before_ref, d_out_ref = take(3)
     grads = [take(info[4]) for info in tasks_info]
@@ -1511,7 +1511,7 @@
         )
 
         def keep(a, slot, value):
-            near_ref[p, a, slot] = value
+            near_ref[p, a, slot] = value + near_before[p, a, slot]
 
         near_sums(rows, sum_ref, keep)
         for i in range(min(pairs, n - 1)):
@@ -1591,7 +1591,7 @@
     run_together(tasks)
 
 
-def back_rows(info, far, diag, q, g, full, kv, peak, dkv, normed_all, normed_own, second, dq_before, d_out, grads,
+def back_rows(info, far, diag, q, g, full, kv, peak, dkv, normed_all, normed_own, second, near_before, dq_before, d_out, grads,
               orders, splits, sizes, rows, collective_id, name="back_rows"):
     seqs, length, double = kv.shape
     width = q.shape[1]
@@ -1602,8 +1602,8 @@
     smem, vmem = pl.BlockSpec(memory_space=pltpu.SMEM), pl.BlockSpec(memory_space=pltpu.VMEM)
     anywhere = pl.BlockSpec(memory_space=pl.ANY)
     bf16, f32 = jnp.bfloat16, jnp.float32
-    ins = [info, far, diag, q, g, full, peak, kv, dkv, normed_all, second]
-    in_specs = [smem, smem] + [vmem] * 5 + [anywhere] * 3 + [vmem]
+    ins = [info, far, diag, q, g, full, peak, kv, dkv, normed_all, second, near_before]
+    in_specs = [smem, smem] + [vmem] * 5 + [anywhere] * 3 + [vmem] * 2
     devices = sizes["x"] * sizes["c"] * n * fast
     own_block = (width // devices, 4 * width)
     inner = None
@@ -1888,6 +1888,7 @@
         normed_all,
         normed_low,
         second,
+        near_before,
         dq_before,
         d_out_w,
         [[wide_pieces[0]] + wide_others, down_half],
@@ -1897,7 +1898,7 @@
         rows,
         5,
     )
-    d_table = bias_grad(near_before + near, rows).reshape(heads * NB)
+    d_table = bias_grad(near, rows).reshape(heads * NB)
     d_queries = jnp.concatenate([dq_before, dq_last], axis=0)
     if joined:
         inner, inner_order = last, "s"

time: 315 us -> 321 us (1.019)
  matrix products: 5.33 us -> 10.8 us
    unnamed x87 -> x81, local copies, waits for them, and re-layouts: 9.2 us -> 8.02 us
  transfers between devices with their start and end apart: 1 -> 1, of which waited for: 1 -> 0; matrix products, arithmetic and copies ran while one was open for 1% -> 1% of each run, Pallas kernels for 6% -> 6%
where the time goes in v3:
time: 321 us; the launch traced here: 316 us
  Pallas kernels  258 us (80%)
  other arithmetic  23.3 us (7%)
  local copies, waits for them, and re-layouts  21.2 us (7%)
  matrix products  10.8 us (3%)
    pallas_call x1, Pallas kernels, back_rows(): pl.pallas_call(functools.partial(back_rows_kernel, sizes, rows, tasks_inf...  75.7 us
    pallas_call x1, Pallas kernels, gather_rows(): pl.pallas_call(functools.partial(gather_rows_kernel, sizes, rows, orders)...  59.4 us
    pallas_call x1, Pallas kernels, gather_all(): pl.pallas_call(functools.partial(gather_kernel, sizes, orders, cuts, int(...  42.7 us
    pallas_call x1, Pallas kernels, reduce_all(): pl.pallas_call(functools.partial(reduce_kernel, sizes, orders, all_dims,...  24.5 us
    pallas_call x1, Pallas kernels, feed_forward(): pl.pallas_call(functools.partial(feed_forward_kernel, sizes), in_specs=[v...  23.7 us
    pallas_call x1, Pallas kernels, attend_back(): pl.pallas_call(functools.partial(attend_back_kernel, rows), grid=(pairs,...  19.5 us
    pallas_call x1, Pallas kernels, attend(): pl.pallas_call(functools.partial(attend_kernel, rows, skip), grid=(pairs,...  10.9 us
    unnamed x81, local copies, waits for them, and re-layouts  8.02 us
  transfers between devices with their start and end apart: 1, of which 0 were waited for; matrix products, arithmetic and copies ran while one was open for 1% of the time, Pallas kernels for 6%

profile of v3, /device:TPU:0, one launch (start us, length us, event | category | flops | bytes accessed | tf_op | source)
XLA Modules:
  0.0 316.3 jit_solution(6511278239664335213)
XLA Ops:
  0.7 0.7 pad_bitcast_fusion
  1.4 0.1 copy.61
  1.5 0.7 copy.59
  2.2 0.7 copy.60
  3.0 1.4 concatenate.23.refs_0_
  4.3 42.7 %gather_first.1 = (bf16[2,2,4,2,16,1152]{5,4,3,2,1,0:T(8,128)(2,1)}, bf16[2,2,4,2,16,1024]{5,4,3,2,1,0:T(8,128)(2,1)}, bf16[4,2,16,4608]{3,2,1,0:T(8,128)(2,1)},...) custom-call(bf16[16,128]{1,0:T(8,128)(2,1)} %concatenate.23.refs_0_, bf16[16,512]{1,0:T(8,128)(2,1)} %refs_1_.1, ...), custom_call_target="tpu_custom_call" | custom-call | tf_op jit(solution)/shard_map/gather_first/pallas_call | solution.py:684
  47.1 0.9 slice.165
  48.0 1.9 fusion.39
  49.9 0.1 copy.69
  50.0 0.7 slice.134
  50.7 0.2 maximum_convert_fusion
  50.9 3.1 add_convert_fusion
  54.0 1.8 multiply_reduce_fusion.11
  55.7 0.1 copy.74
  55.9 0.2 multiply_convert_fusion.refs_12_
  56.1 2.5 convolution_convert_fusion.1.refs_4_.q_ref.refs_3_
  58.7 0.1 reshape.236
  58.8 0.2 fusion.31
  59.0 0.6 reshape.237.refs_2_.diag_ref
  59.6 0.7 pad_maximum_fusion.refs_1_.far_ref
  60.3 0.6 pad_add_fusion.1.refs_0_.info_ref
  60.9 59.4 %gather_rows.1 = (bf16[2,2,4,2,16,4608]{5,4,3,2,1,0:T(8,128)(2,1)}, bf16[2,2,4,2,64,512]{5,4,3,2,1,0:T(8,128)(2,1)}, bf16[2,4,2,256,512]{4,3,2,1,0:T(8,128)(2,1)...) custom-call(s32[3]{0:T(128)} %pad_add_fusion.1.refs_0_.info_ref, ...), custom_call_target="tpu_custom_call" | custom-call | tf_op jit(solution)/shard_map/gather_rows/pallas_call | solution.py:802
  120.4 10.9 %attend.1 = (bf16[256,512]{1,0:T(8,128)(2,1)S(1)}, f32[256,512]{1,0:T(8,128)S(1)}, f32[256,512]{1,0:T(8,128)S(1)}, f32[1,4,2,256]{3,2,1,0:T(2,128)S(1)}) custom-call(s32[3]{0:T(128)S(1)} %copy-done.21, f32[8,2]{1,0:T(8,128)S(1)} %copy-done.15, f32[4,6,512]{2,1,0:T(8,128)S(1)} %copy-done.1, bf16[512,512]{1,0:T(8,128)(2,1)S(1)} %copy-done, ...), custom_call_target="tpu_custom_call" | custom-call | flops 4294967296 | bytes 8912896 | tf_op jit(solution)/shard_map/attend/pallas_call | solution.py:215
  131.3 0.8 copy-done.5
  132.1 0.8 copy-done.8
  132.9 0.7 copy-done.9
  133.6 0.6 copy-done.20
  134.2 0.1 copy.72
  134.3 0.6 bitcast_convert_fusion.refs_4_
  134.9 23.7 %feed_forward.1 = (bf16[512,512]{1,0:T(8,128)(2,1)}, f32[512,512]{1,0:T(8,128)}, bf16[512,512]{1,0:T(8,128)(2,1)}, bf16[512,512]{1,0:T(8,128)(2,1)}, f32[1,512]{...) custom-call(f32[512,512]{1,0:T(8,128)} %copy-done.24, ...), custom_call_target="tpu_custom_call" | custom-call | tf_op jit(solution)/shard_map/feed_forward/pallas_call | solution.py:1365
  158.6 1.8 collective-permute-start
  160.4 0.6 compare_reduce_fusion
  161.1 1.0 iota_compare_fusion
  162.1 0.7 convert.28
  162.8 1.0 copy-done.6
  163.8 19.5 %attend_back.1 = (bf16[256,512]{1,0:T(8,128)(2,1)S(1)}, bf16[1,2048,1024]{2,1,0:T(8,128)(2,1)}, f32[4,2,5,8,512]{4,3,2,1,0:T(8,128)S(1)}) custom-call(s32[3]{0:T(128)S(1)} %copy-done.21, f32[8,2]{1,0:T(8,128)S(1)} %copy-done.15, f32[4,6,512]{2,1,0:T(8,128)S(1)} %copy-done.1, bf16[512,512]{1,0:T(8,128)(2,1)S(1)} %copy-done, bf16[512,512]{1,0:T(8,128)(2,1)S(1)} %copy-done.6, ...), custom_call_target="tpu_custom_call" | custom-call | flops 12884901888 | bytes 26738688 | tf_op jit(solution)/shard_map/attend_back/pallas_call | solution.py:343
  183.3 0.7 copy-done.2
  184.0 0.9 copy-done.4
  184.8 75.7 %back_rows.1 = (f32[2,256,512]{2,1,0:T(8,128)}, bf16[256,512]{1,0:T(8,128)(2,1)}, f32[4,2,5,8,512]{4,3,2,1,0:T(8,128)}, f32[16,2048]{1,0:T(8,128)}, f32[16,2048]...) custom-call(s32[3]{0:T(128)} %pad_add_fusion.1.refs_0_.info_ref, ...), custom_call_target="tpu_custom_call" | custom-call | tf_op jit(solution)/shard_map/back_rows/pallas_call | solution.py:1661
  260.5 1.8 slice.186
  262.4 1.1 slice_reduce_fusion
  263.5 2.5 multiply_reduce_fusion
  266.1 0.3 fusion.19
  266.4 2.6 fusion.26
  269.0 1.3 convolution_convert_fusion
  270.4 2.5 select_reduce_fusion
  272.9 0.7 add_select_fusion
  273.8 0.1 scatter-add.9
  274.0 0.1 reshape.251
  274.1 5.4 %multiply_reduce_fusion.9 = (f32[512]{0:T(512)S(1)}, f32[512]{0:T(512)S(1)}, f32[512]{0:T(512)S(1)}, f32[512]{0:T(512)S(1)}, f32[512]{0:T(512)S(1)}, /*index=5*/...) fusion(f32[2,259,512]{2,1,0:T(8,128)S(1)} %maximum_convert_fusi, ...), kind=kLoop, calls=%fused_computation.45 | loop fusion | flops 20442624 | bytes 10508288 | tf_op jit(solution)/shard_map/transpose(jvp())/reduce_sum | solution.py:63
  279.6 1.1 fusion.20
  280.7 1.1 copy.68
  281.8 0.3 broadcast_multiply_fusion.7
  282.1 0.9 copy-done.30
  283.0 0.3 copy-done.31
  283.3 0.9 broadcast_multiply_fusion
  284.2 1.2 pad_add_fusion
  285.4 0.6 slice.189.refs_2_
  286.0 24.5 %reduce.21 = (f32[16,512]{1,0:T(8,128)}, f32[16,128]{1,0:T(8,128)}, f32[16,512]{1,0:T(8,128)}, f32[16,512]{1,0:T(8,128)}, f32[16,1024]{1,0:T(8,128)}, /*index=5*/f32[2,8,512]{2,1,0:T(8,128)}) custom-call(bf16[2,2,4,2,16,640]{5,4,3,2,1,0:T(8,128)(2,1)} %bitcast.70, bf16[4,2,16,2048]{3,2,1,0:T(8,128)(2,1)} %get-tuple-element.141.refs_1_, ...), custom_call_target="tpu_custom_call" | custom-call | tf_op jit(solution)/shard_map/reduce/pallas_call | solution.py:1115
  310.6 1.5 slice_reduce_fusion.3
  312.0 1.4 slice_reduce_fusion.5
  313.5 0.2 slice_add_fusion.refs_1_
  313.7 0.7 copy-done.7
  314.6 1.3 finish.1
  (86 shorter events, 0.9 us)
Async XLA Ops:
  0.6 50.1 %copy-start.27 = (bf16[2,256,512]{2,1,0:T(8,128)(2,1)S(1)}, bf16[2,256,512]{2,1,0:T(8,128)(2,1)}, u32[]{:S(2)}) copy-start(bf16[2,256,512]{2,1,0:T(8,128)(2,1)} %refs_15_.1) | copy-start | bytes 1572868
  54.0 1.8 copy-start.28
  55.7 2.9 copy-start.24
  56.0 4.9 %copy-start.26 = (bf16[512,512]{1,0:T(8,128)(2,1)}, bf16[512,512]{1,0:T(8,128)(2,1)S(1)}, u32[]{:S(2)}) copy-start(bf16[512,512]{1,0:T(8,128)(2,1)S(1)} %multiply_convert_fusion.refs_12_) | copy-start | bytes 1572868
  56.0 2.8 copy-start.37
  56.1 4.3 %copy-start.38 = (s32[2]{0:T(128)S(1)}, s32[2]{0:T(128)}, u32[]{:S(2)}) copy-start(s32[2]{0:T(128)} %param.22) | copy-start | bytes 28
  60.9 59.5 %copy-start = (bf16[512,512]{1,0:T(8,128)(2,1)S(1)}, bf16[512,512]{1,0:T(8,128)(2,1)}, u32[]{:S(2)}) copy-start(bf16[512,512]{1,0:T(8,128)(2,1)} %convolution_convert_fusion.1.refs_4_.q_ref.refs_3_) | copy-start | bytes 1572868
  60.9 59.5 %copy-start.1 = (f32[4,6,512]{2,1,0:T(8,128)S(1)}, f32[4,6,512]{2,1,0:T(8,128)}, u32[]{:S(2)}) copy-start(f32[4,6,512]{2,1,0:T(8,128)} %reshape.237.refs_2_.diag_ref) | copy-start | bytes 147460
  60.9 59.5 %copy-start.15 = (f32[8,2]{1,0:T(8,128)S(1)}, f32[8,2]{1,0:T(8,128)}, u32[]{:S(2)}) copy-start(f32[8,2]{1,0:T(8,128)} %pad_maximum_fusion.refs_1_.far_ref) | copy-start | bytes 196
  60.9 59.5 %copy-start.21 = (s32[3]{0:T(128)S(1)}, s32[3]{0:T(128)}, u32[]{:S(2)}) copy-start(s32[3]{0:T(128)} %pad_add_fusion.1.refs_0_.info_ref) | copy-start | bytes 40
  120.4 13.8 %copy-start.34 = (bf16[512,1]{1,0:T(8,128)(2,1)S(1)}, bf16[512,1]{1,0:T(8,128)(2,1)}, u32[]{:S(2)}) copy-start(bf16[512,1]{1,0:T(8,128)(2,1)} %get-tuple-element.188) | copy-start | bytes 3076
  131.3 0.8 copy-start.5
  132.1 0.8 copy-start.8
  132.9 0.7 copy-start.9
  133.6 0.6 copy-start.20
  134.9 26.2 %copy-start.36 = (s32[3,8,512]{2,1,0:T(8,128)S(1)}, s32[3,8,512]{2,1,0:T(8,128)}, u32[]{:S(2)}) copy-start(s32[3,8,512]{2,1,0:T(8,128)} %constant.236) | copy-start | bytes 147460
  134.9 27.8 %copy-start.22 = (f32[256,512]{1,0:T(8,128)S(1)}, f32[256,512]{1,0:T(8,128)}, u32[]{:S(2)}) copy-start(f32[256,512]{1,0:T(8,128)} %get-tuple-element.123.full_ref) | copy-start | bytes 1572868
  134.9 27.8 %copy-start.23 = (f32[1,4,2,256]{3,2,1,0:T(2,128)S(1)}, f32[1,4,2,256]{3,2,1,0:T(2,128)}, u32[]{:S(2)}) copy-start(f32[1,4,2,256]{3,2,1,0:T(2,128)} %get-tuple-element.124.peak_ref) | copy-start | bytes 24580
  158.6 26.2 %collective-permute-start = (bf16[4,2,16,4096]{3,2,1,0:T(8,128)(2,1)}, bf16[4,2,16,4096]{3,2,1,0:T(8,128)(2,1)}, u32[]{:S(2)}, u32[]{:S(2)}) collective-permute-start(bf16[4,2,16,4096]{3,2,1,0:T(8,128)(2,1)} %get-tuple-element.128), channel_id=1, source_target_pairs={{16,0},{24,8},{0,16},{8,24},{17,1},{25,9},{1,17},{9,25},{18,2},{26... | collective-permute-start | bytes 3145736 | tf_op jit(solution)/shard_map/ppermute | solution.py:1403
  162.8 1.0 copy-start.6
  183.3 0.7 copy-start.2
  184.0 0.9 copy-start.4
  260.5 3.0 copy-start.3
  260.5 3.0 copy-start.35
  263.5 2.6 copy-start.25
  263.5 2.6 copy-start.33
  266.4 2.6 copy-start.29
  269.0 1.4 copy-start.32
  281.8 1.2 copy-start.30
  281.8 1.5 copy-start.31
  313.4 1.0 copy-start.7
  313.4 1.1 copy-start.10
  313.4 1.1 copy-start.11
  313.4 1.1 copy-start.12
  313.4 1.1 copy-start.13
  313.4 1.1 copy-start.14
  313.4 1.1 copy-start.16
  313.4 1.1 copy-start.17
  313.5 1.1 copy-start.18
  313.5 1.1 copy-start.19
